TPU v7x, 128 devices: a whole 4x4x4 slice. The times are simulated.
128 devices in a mesh: lon: 32 (over z_lo, y, x), lat: 4 (over z_hi, core).
Axes of the slice: x: 4, y: 4, z: 4 (z_hi: 2, z_lo: 2; z = z_hi * 2 + z_lo), core: 2. Of those that a mesh axis runs over, the one named last changes fastest.
Arguments:
- tokens: bfloat16 [6, 288, 768, 192], P(None, 'lat', 'lon'), may hold values from -6 to 6
- obs_values: bfloat16 [262144, 256], P(('lon', 'lat')), may hold values from -6 to 6
- obs_dest: int32 [262144], P(('lon', 'lat')), may hold values from 0 to 127, as said below
- obs_cell: int32 [262144], P(('lon', 'lat')), may hold values from 0 to 10367
- obs_count: int32 [128], P(('lon', 'lat')), may hold values from 1365 to 2048, as said below
- w_obs: bfloat16 [256, 192], replicated, may hold values from -0.375 to 0.375
- ln1_gain: float32 [192], replicated, may hold values from 0.1 to 1.9
- w_qkv: bfloat16 [192, 576], replicated, may hold values from -0.4375 to 0.4375
- position_bias: float32 [6, 144, 144], replicated, may hold values from -4 to 400
- w_proj: bfloat16 [192, 192], replicated, may hold values from -0.4375 to 0.4375
- ln2_gain: float32 [192], replicated, may hold values from 0.1 to 1.9
- w_up: bfloat16 [192, 768], replicated, may hold values from -0.4375 to 0.4375
- w_down: bfloat16 [768, 192], replicated, may hold values from -0.21875 to 0.21875
Outputs:
- block_out: bfloat16 [6, 288, 768, 192], P(None, 'lat', 'lon')
Inputs may be any that keep to these rules, and one draw needn't show every extreme that they name: `obs_dest`: the tile owning a row, numbered lon index * 4 + lat index; among the live rows of one device no tile is named more than 32 times, and in every draw one tile is named exactly 32 times by the live rows of every device. `obs_cell`: a cell of the owning tile, numbered (level * 72 + row) * 24 + column. The live rows of device s are the first obs_count[s] rows of its block; the others are padding.
All inputs are finite; a program needn't handle non-finite values.
Results may differ from a plain program's by a relative error of at most 0.01.
Values may be sent and summed in bfloat16 or wider, within the bound.
A program may use at most 128 MiB of HBM per device.

v0:
```python
import math

import jax
import jax.numpy as jnp
import numpy as np
from jax import lax
from jax.experimental import pallas as pl
from jax.experimental.pallas import tpu as pltpu
from jax.sharding import PartitionSpec as P

WZ = 2
WLAT = 6
WLON = 12
F32=jnp.float32; BF=jnp.bfloat16
WIN=144; D=192; HEADS=6; HD=32
NT=(((1,),(1,)),((),()))
LOG2E=math.log2(math.e)

def dot(a,b): return jnp.dot(a,b,preferred_element_type=F32)
def dot_nt(a,b): return lax.dot_general(a,b,NT,preferred_element_type=F32)

def norm(x, gain):
    mean=jnp.mean(x,axis=-1,keepdims=True)
    c=x-mean
    var=jnp.mean(c*c,axis=-1,keepdims=True)
    return (c*lax.rsqrt(var+1e-5)*gain).astype(BF)

def gelu(x):
    h=0.5*x
    return h+h*lax.erf(x*np.float32(math.sqrt(0.5)))

def head_mask(shape, h, width=HD):
    lane=lax.broadcasted_iota(jnp.int32,shape,len(shape)-1)
    return (lane>=h*width)&(lane<(h+1)*width)

GROUPS=((0,4,0,128),(4,2,128,64))

def kernel(edge_ref, x_ref, bias_ref, g1_ref, wqkv_ref, wp_ref, g2_ref, wup_ref, wdnt_ref, o_ref, xs, s_ref, p_ref, ctx_ref):
    band=pl.program_id(0)
    lat_edge=jnp.where(band==pl.num_programs(0)-1, edge_ref[0], 0)
    zero=jnp.zeros((),BF)
    def pair(k,_):
        lvls=(2*k+1, lax.rem(2*k+2,6))
        for i in range(2):
            for r in range(6):
                row=x_ref[lvls[i], r].astype(F32)
                for w in range(2):
                    base=w*WIN+(i*6+r)*12
                    xs[base:base+12,:]=row[w*12:w*12+12]
        lvl_edge=(k==2).astype(jnp.int32)
        var=2*lat_edge+lvl_edge
        n1=norm(xs[...],g1_ref[...])
        q_all=(dot(n1,wqkv_ref[:,0:256])*np.float32(LOG2E/math.sqrt(HD))).astype(BF)
        k_all=dot(n1,wqkv_ref[:,256:512]).astype(BF)
        v_all=dot(n1,wqkv_ref[:,512:768]).astype(BF)
        for w in range(2):
            sl=slice(w*WIN,(w+1)*WIN)
            for h0,nh,l0,ln in GROUPS:
                qg=q_all[sl,l0:l0+128]; kg=k_all[sl,l0:l0+128]
                qs=jnp.concatenate([jnp.where(head_mask((WIN,128),h),qg,zero) for h in range(nh)],axis=0)
                s_ref[w,h0*WIN:(h0+nh)*WIN,:]=dot_nt(qs,kg)
        for w in range(2):
            sl=slice(w*WIN,(w+1)*WIN)
            ls=[]
            for h in range(HEADS):
                s=s_ref[w,h*WIN:(h+1)*WIN,:]+bias_ref[var,h*WIN:(h+1)*WIN,:]
                m=jnp.max(s,axis=-1,keepdims=True)
                p=jnp.exp2(s-m)
                ls.append(jnp.sum(p,axis=-1,keepdims=True))
                p_ref[w,h*WIN:(h+1)*WIN,:]=p.astype(BF)
            for h0,nh,l0,ln in GROUPS:
                o=dot(p_ref[w,h0*WIN:(h0+nh)*WIN,:],v_all[sl,l0:l0+128])
                c=o[:WIN]; l=ls[h0]*jnp.ones((1,128),F32)
                for h in range(1,nh):
                    mk=head_mask((WIN,128),h)
                    c=jnp.where(mk,o[h*WIN:(h+1)*WIN],c)
                    l=jnp.where(mk,ls[h0+h],l)
                ctx_ref[sl,l0:l0+128]=(c*(1.0/l)).astype(BF)
        att=(xs[...]+dot(ctx_ref[:,:D],wp_ref[...])).astype(BF).astype(F32)
        n2=norm(att,g2_ref[...])
        acc=att
        for j in range(3):
            hid=gelu(dot(n2,wup_ref[:,j*256:(j+1)*256])).astype(BF)
            acc=acc+dot_nt(hid,wdnt_ref[:,j*256:(j+1)*256])
        xs[...]=acc
        for i in range(2):
            for r in range(6):
                for w in range(2):
                    base=w*WIN+(i*6+r)*12
                    o_ref[lvls[i], r, w*12:w*12+12,:]=xs[base:base+12,:].astype(BF)
        return 0
    lax.fori_loop(0,3,pair,0)

def prep_bias(position_bias):
    b=position_bias*np.float32(LOG2E)
    lvl=np.arange(WIN)//72; row=np.arange(WIN)//12%6
    outs=[]
    for le in range(2):
        for ve in range(2):
            g=2*le*(row>=3)+ve*lvl
            outs.append((g[:,None]!=g[None,:]).astype(np.float32)*np.float32(-1e30))
    return (b[None]+jnp.asarray(np.stack(outs))[:,None]).reshape(4,HEADS*WIN,WIN)

def compute(shifted, lat_edge, position_bias, g1, wqkv, wp, g2, wup, wdn):
    bias=prep_bias(position_bias)
    wq=jnp.pad(wqkv.reshape(D,3,D),((0,0),(0,0),(0,64))).reshape(D,768)
    full=lambda *s: pl.BlockSpec(s,lambda i:(0,)*len(s),pipeline_mode=pl.Buffered(1))
    return pl.pallas_call(
        kernel, grid=(12,),
        in_specs=[pl.BlockSpec(memory_space=pltpu.SMEM),
          pl.BlockSpec((6,6,24,D),lambda i:(0,i,0,0)),
          full(4,HEADS*WIN,WIN),full(1,D),full(D,768),full(D,D),full(1,D),full(D,768),full(D,768)],
        out_specs=pl.BlockSpec((6,6,24,D),lambda i:(0,i,0,0)),
        out_shape=jax.ShapeDtypeStruct((6,72,24,D),BF),
        scratch_shapes=[pltpu.VMEM((2*WIN,D),F32),pltpu.VMEM((2,HEADS*WIN,WIN),F32),pltpu.VMEM((2,HEADS*WIN,WIN),BF),pltpu.VMEM((2*WIN,256),BF)],
        compiler_params=pltpu.CompilerParams(vmem_limit_bytes=56<<20),
    )(lat_edge,shifted,bias,g1.reshape(1,D),wq,wp,g2.reshape(1,D),wup,wdn.T)


def passed_along(block, axis, distance):
    devices = range(lax.axis_size(axis))
    route = [((i - distance) % len(devices), i) for i in devices]
    return lax.ppermute(block, axis, route)


def on_device(
    tokens,
    obs_values,
    obs_dest,
    obs_cell,
    obs_count,
    w_obs,
    ln1_gain,
    w_qkv,
    position_bias,
    w_proj,
    ln2_gain,
    w_up,
    w_down,
):
    levels, lat_rows, lon_cols, features = tokens.shape
    lon_count = lax.axis_size("lon")
    lat_count = lax.axis_size("lat")
    devices = lon_count * lat_count
    row_count = obs_values.shape[0]
    capacity = 2 * row_count // devices
    position = jnp.arange(row_count, dtype=jnp.int32)
    is_live = position < obs_count[0]
    matches = (
        (obs_dest[:, None] == jnp.arange(devices, dtype=jnp.int32)[None, :]) & is_live[:, None]
    ).astype(jnp.int32)
    earlier = jnp.cumsum(matches, axis=0) - matches
    slot_ids = jnp.sum(earlier * matches, axis=1)
    targets = jnp.where(is_live, obs_dest * capacity + slot_ids, devices * capacity)
    cell_ids = jnp.zeros((devices * capacity,), jnp.int32).at[targets].set(obs_cell, mode="drop")
    payload = jnp.dot(obs_values, w_obs, preferred_element_type=jnp.float32).astype(jnp.bfloat16)
    buffer = (
        jnp.zeros((devices * capacity, payload.shape[1]), jnp.bfloat16)
        .at[targets]
        .set(payload, mode="drop")
    )
    received, got_cells = (
        lax.all_to_all(buffer, ("lon", "lat"), split_axis=0, concat_axis=0, tiled=True),
        lax.all_to_all(cell_ids, ("lon", "lat"), split_axis=0, concat_axis=0, tiled=True),
    )
    obs_field = (
        jnp.zeros((levels * lat_rows * lon_cols, features), jnp.float32)
        .at[got_cells]
        .add(received.astype(jnp.float32))
    )
    stream = (tokens.astype(jnp.float32) + obs_field.reshape(tokens.shape)).astype(jnp.bfloat16)
    half_lat = WLAT // 2
    half_lon = WLON // 2
    lat_index = lax.axis_index("lat")
    arrived = passed_along(stream[:, :, :half_lon], "lon", -1)
    widened = jnp.concatenate([stream[:, :, half_lon:], arrived], axis=2)
    arrived = passed_along(widened[:, :half_lat], "lat", -1)
    shifted = jnp.concatenate([widened[:, half_lat:], arrived], axis=1)
    edge = (lat_index == lat_count - 1).astype(jnp.int32).reshape(1)
    result = compute(
        shifted, edge, position_bias, ln1_gain, w_qkv, w_proj, ln2_gain, w_up, w_down
    )
    arrived = passed_along(result[:, lat_rows - half_lat :], "lat", 1)
    widened = jnp.concatenate([arrived, result[:, : lat_rows - half_lat]], axis=1)
    arrived = passed_along(widened[:, :, lon_cols - half_lon :], "lon", 1)
    return jnp.concatenate([arrived, widened[:, :, : lon_cols - half_lon]], axis=2)


def solution(mesh):
    in_specs = (
        P(None, "lat", "lon", None),
        P(("lon", "lat"), None),
        P(("lon", "lat")),
        P(("lon", "lat")),
        P(("lon", "lat")),
        P(),
        P(),
        P(),
        P(),
        P(),
        P(),
        P(),
        P(),
    )
    out_specs = P(None, "lat", "lon", None)
    return jax.shard_map(
        on_device, mesh=mesh, in_specs=in_specs, out_specs=out_specs, check_vma=False
    )
```

profile of v0, /device:TPU:1, one launch (start us, length us, event | category | flops | bytes accessed | tf_op | source)
XLA Modules:
  0.0 276.1 jit_solution(5551044526959569841)
XLA Ops:
  0.8 0.8 copy.20
  1.6 0.6 fusion.9
  2.2 0.1 broadcast_add_fusion
  2.3 0.3 copy.21
  2.7 0.0 copy-done.6
  2.7 1.1 fusion.6
  3.8 8.2 %scatter_custom_fusion = s32[4096]{0:T(1024)S(1)} fusion(s32[2048]{0:T(1024)S(1)} %compare_select_fusion.1, s32[2048]{0:T(1024)} %param.17, s32[]{:T(128)} %constant.14.clone.1), kind=kCustom, calls=%fused_computation.37 | custom fusion | bytes 16896 | tf_op jit(solution)/shard_map/scatter | solution.py:155
  12.1 0.7 all_to_all.14
  12.8 11.5 %all-to-all-start = ((s32[128,32,1]{1,2,0:T(1,128)}), s32[128,32,1]{1,2,0:T(1,128)S(1)}, u32[]{:S(2)}, u32[]{:S(2)}) async-start(s32[128,32,1]{1,2,0:T(1,128)} %bitcast.6), calls=%async_computation | async-start | bytes 131072 | tf_op jit(solution)/shard_map/all_to_all | solution.py:164
  24.3 0.5 convolution_convert_fusion
  24.8 0.5 copy.23
  25.3 10.9 %scatter_custom_fusion.1 = bf16[4096,192]{1,0:T(8,128)(2,1)} fusion(s32[2048]{0:T(1024)S(1)} %compare_select_fusion.1, bf16[2048,192]{1,0:T(8,128)(2,1)S(1)} %copy.23, bf16[]{:T(256)} %constant.30.clone.1), kind=kCustom, calls=%fused_computation.19 | custom fusion | bytes 1572866 | tf_op jit(solution)/shard_map/scatter | solution.py:160
  36.2 0.0 all-to-all-done
  36.2 9.8 %all-to-all-start.1 = ((bf16[128,32,192]{2,1,0:T(8,128)(2,1)}), bf16[128,32,192]{2,1,0:T(8,128)(2,1)S(1)}, u32[]{:S(2)}, u32[]{:S(2)}) async-start(bf16[128,32,192]{2,1,0:T(8,128)(2,1)} %bitcast.35), calls=%async_computation.1 | async-start | bytes 4194304 | tf_op jit(solution)/shard_map/all_to_all | solution.py:163
  46.0 0.6 broadcast.67
  46.6 0.8 reduce.3
  47.4 0.1 all_to_all.16
  47.6 28.4 %all-to-all-done.1 = bf16[128,32,192]{2,1,0:T(8,128)(2,1)S(1)} async-done(((bf16[128,32,192]{2,1,0:T(8,128)(2,1)}), bf16[128,32,192]{2,1,0:T(8,128)(2,1)S(1)}, u32[]{:S(2)}, u32[]{:S(2)}) %all-to-all-start.1) | async-done | bytes 1572896 | tf_op jit(solution)/shard_map/all_to_all | solution.py:163
  76.0 28.1 %scatter_custom_fusion.2 = f32[10368,192]{1,0:T(8,128)} fusion(s32[4096]{0:T(1024)S(1)} %bitcast.41, f32[]{:T(128)} %constant.13.clone.1, bf16[4096,192]{1,0:T(8,128)(2,1)S(1)} %bitcast.34), kind=kCustom, calls=%fused_computation.9 | custom fusion | flops 1572864 | bytes 10059780 | tf_op jit(solution)/shard_map/scatter-add | solution.py:169
  104.0 9.1 %add_convert_fusion = bf16[6,72,24,192]{3,2,1,0:T(8,128)(2,1)} fusion(f32[6,72,24,192]{3,2,1,0:T(8,128)} %bitcast.33, bf16[6,72,24,192]{3,2,1,0:T(8,128)(2,1)} %param.14), kind=kLoop, calls=%fused_computation.3 | loop fusion | flops 5971968 | bytes 15925248 | tf_op jit(solution)/shard_map/convert_element_type | solution.py:171
  113.2 1.7 slice.43
  114.9 0.3 copy.24
  115.2 0.5 collective-permute-start
  115.7 0.0 copy-done.4
  115.7 0.2 copy.26
  115.9 0.9 copy.30.wqkv_ref
  116.8 0.1 broadcast_multiply_fusion
  116.9 3.4 %bitcast_add_fusion.bias_ref = f32[4,864,144]{2,1,0:T(8,128)} fusion(f32[4,144,144]{2,1,0:T(8,128)} %constant.32.clone, f32[864,144]{1,0:T(8,128)S(1)} %bitcast.36), kind=kLoop, calls=%fused_computation.13 | loop fusion | flops 497664 | bytes 2820096 | tf_op jit(solution)/shard_map/add | solution.py:102
  120.3 3.1 %slice.42 = bf16[6,72,18,192]{3,2,1,0:T(8,128)(2,1)S(1)} slice(bf16[6,72,24,192]{3,2,1,0:T(8,128)(2,1)S(1)} %copy-done.2), slice={[0:6], [0:72], [6:24], [0:192]} | slice | bytes 5971968 | tf_op jit(solution)/shard_map/slice | solution.py:176
  123.4 22.5 %collective-permute-done = bf16[6,72,6,192]{3,1,2,0:T(8,128)(2,1)} collective-permute-done((bf16[6,72,6,192]{3,1,2,0:T(8,128)(2,1)S(1)}, bf16[6,72,6,192]{3,1,2,0:T(8,128)(2,1)}, u32[]{:S(2)}, u32[]{:S(2)}) %collective-permute-start) | collective-permute-done | bytes 995360 | tf_op jit(solution)/shard_map/ppermute | solution.py:123
  145.9 1.7 copy.25
  147.6 0.1 pad_maximum_fusion.3
  147.6 0.5 collective-permute-start.1
  148.1 2.1 fusion.3
  150.2 4.4 %collective-permute-done.1 = bf16[6,3,24,192]{3,2,1,0:T(8,128)(2,1)S(1)} collective-permute-done((bf16[6,3,24,192]{3,2,1,0:T(8,128)(2,1)S(1)}, bf16[6,3,24,192]{3,2,1,0:T(8,128)(2,1)S(1)}, u32[]{:S(2)}, u32[]{:S(2)}) %collective-permute-start.1) | collective-permute-done | bytes 165920 | tf_op jit(solution)/shard_map/ppermute | solution.py:123
  154.6 3.2 %pad_maximum_fusion.1.x_ref = bf16[6,72,24,192]{3,2,1,0:T(8,128)(2,1)} fusion(bf16[6,3,24,192]{3,2,1,0:T(8,128)(2,1)S(1)} %collective-permute-done.1, bf16[6,69,24,192]{3,2,1,0:T(8,128)(2,1)S(1)} %fusion.3), kind=kLoop, calls=%fused_computation.8 | loop fusion | flops 1990656 | bytes 7962624 | tf_op jit(solution)/shard_map/concatenate | solution.py:178
  157.8 74.7 %shard_map.136 = bf16[6,72,24,192]{3,2,1,0:T(8,128)(2,1)} custom-call(s32[1]{0:T(128)} %bitcast.edge_ref, bf16[6,72,24,192]{3,2,1,0:T(8,128)(2,1)} %pad_maximum_fusion.1.x_ref, f32[4,864,144]{2,1,0:T(8,128)} %bitcast_add_fusion.bias_ref, f32[1,192]{1,0:T(1,128)} %bitcast.42, bf16[192,768]{1,0:T(8,128)(2,1)} %copy.30.wqkv_ref, bf16[192,192]{1,0:T(8,128)(2,1)} %wp_ref.1, ...), custom_call_target="tpu_custom_call" | custom-call | tf_op jit(solution)/shard_map/pallas_call | solution.py:108
  232.5 1.0 slice.46
  233.5 0.1 collective-permute-start.2
  233.5 2.8 %slice.47 = bf16[6,69,24,192]{3,2,1,0:T(8,128)(2,1)S(1)} slice(bf16[6,72,24,192]{3,2,1,0:T(8,128)(2,1)} %shard_map.136), slice={[0:6], [0:69], [0:24], [0:192]} | slice | bytes 7630848 | tf_op jit(solution)/shard_map/slice | solution.py:184
  236.3 0.1 collective-permute-done.2
  236.4 0.5 pad_maximum_fusion.2
  236.9 0.3 copy.28
  237.2 0.1 collective-permute-start.3
  237.3 33.8 %collective-permute-done.3 = bf16[6,72,6,192]{3,1,2,0:T(8,128)(2,1)S(1)} collective-permute-done((bf16[6,72,6,192]{3,1,2,0:T(8,128)(2,1)S(1)}, bf16[6,72,6,192]{3,1,2,0:T(8,128)(2,1)S(1)}, u32[]{:S(2)}, u32[]{:S(2)}) %collective-permute-start.3) | collective-permute-done | bytes 995360 | tf_op jit(solution)/shard_map/ppermute | solution.py:123
  271.0 0.4 copy.29
  271.4 4.6 %fusion = bf16[6,72,24,192]{3,2,1,0:T(8,128)(2,1)} fusion(bf16[6,69,24,192]{3,2,1,0:T(8,128)(2,1)S(1)} %slice.47, bf16[6,3,24,192]{3,2,1,0:T(8,128)(2,1)S(1)} %collective-permute-done.2, bf16[6,72,6,192]{3,2,1,0:T(8,128)(2,1)S(1)} %copy.29), kind=kLoop, calls=%fused_computation.5 | loop fusion | flops 11943936 | bytes 8957952 | tf_op jit(solution)/shard_map/concatenate | solution.py:186
  276.1 0.0 copy-done.1
  (19 shorter events, 0.2 us)
Async XLA Ops:
  0.0 24.3 %copy-start = (bf16[2048,256]{1,0:T(8,128)(2,1)S(1)}, bf16[2048,256]{1,0:T(8,128)(2,1)}, u32[]{:S(2)}) copy-start(bf16[2048,256]{1,0:T(8,128)(2,1)} %param.15) | copy-start | bytes 3145732
  0.0 2.7 copy-start.6
  0.0 24.3 %copy-start.5 = (bf16[256,192]{0,1:T(8,128)(2,1)S(1)}, bf16[256,192]{0,1:T(8,128)(2,1)}, u32[]{:S(2)}) copy-start(bf16[256,192]{0,1:T(8,128)(2,1)} %param.19) | copy-start | bytes 294916
  12.8 23.4 %all-to-all-start = ((s32[128,32,1]{1,2,0:T(1,128)}), s32[128,32,1]{1,2,0:T(1,128)S(1)}, u32[]{:S(2)}, u32[]{:S(2)}) async-start(s32[128,32,1]{1,2,0:T(1,128)} %bitcast.6), calls=%async_computation | async-start | bytes 131072 | tf_op jit(solution)/shard_map/all_to_all | solution.py:164
  36.2 39.8 %all-to-all-start.1 = ((bf16[128,32,192]{2,1,0:T(8,128)(2,1)}), bf16[128,32,192]{2,1,0:T(8,128)(2,1)S(1)}, u32[]{:S(2)}, u32[]{:S(2)}) async-start(bf16[128,32,192]{2,1,0:T(8,128)(2,1)} %bitcast.35), calls=%async_computation.1 | async-start | bytes 4194304 | tf_op jit(solution)/shard_map/all_to_all | solution.py:163
  113.2 2.5 copy-start.4
  113.2 3.6 %copy-start.3 = (f32[6,144,144]{2,1,0:T(8,128)S(1)}, f32[6,144,144]{2,1,0:T(8,128)}, u32[]{:S(2)}) copy-start(f32[6,144,144]{2,1,0:T(8,128)} %param.22) | copy-start | bytes 1492996
  115.2 30.7 %collective-permute-start = (bf16[6,72,6,192]{3,1,2,0:T(8,128)(2,1)S(1)}, bf16[6,72,6,192]{3,1,2,0:T(8,128)(2,1)}, u32[]{:S(2)}, u32[]{:S(2)}) collective-permute-start(bf16[6,72,6,192]{3,1,2,0:T(8,128)(2,1)S(1)} %copy.24), channel_id=1, source_target_pairs={{4,0},{8,4},{12,8},{16,12},{20,16},{24,20},{28,24},{32,28},{36,32}... | collective-permute-start | bytes 2985992 | tf_op jit(solution)/shard_map/ppermute | solution.py:123
  116.8 3.5 %copy-start.2 = (bf16[6,72,24,192]{3,2,1,0:T(8,128)(2,1)S(1)}, bf16[6,72,24,192]{3,2,1,0:T(8,128)(2,1)}, u32[]{:S(2)}) copy-start(bf16[6,72,24,192]{3,2,1,0:T(8,128)(2,1)} %add_convert_fusion) | copy-start | bytes 11943940
  147.6 6.9 %collective-permute-start.1 = (bf16[6,3,24,192]{3,2,1,0:T(8,128)(2,1)S(1)}, bf16[6,3,24,192]{3,2,1,0:T(8,128)(2,1)S(1)}, u32[]{:S(2)}, u32[]{:S(2)}) collective-permute-start(bf16[6,3,24,192]{3,2,1,0:T(8,128)(2,1)S(1)} %pad_maximum_fusion.3), channel_id=1, source_target_pairs={{1,0},{2,1},{3,2},{0,3},{5,4},{6,5},{7,6},{4,7},{9,8},{10,9},{11,1... | collective-permute-start | bytes 497672 | tf_op jit(solution)/shard_map/ppermute | solution.py:123
  233.5 3.0 %collective-permute-start.2 = (bf16[6,3,24,192]{3,2,1,0:T(8,128)(2,1)S(1)}, bf16[6,3,24,192]{3,2,1,0:T(8,128)(2,1)S(1)}, u32[]{:S(2)}, u32[]{:S(2)}) collective-permute-start(bf16[6,3,24,192]{3,2,1,0:T(8,128)(2,1)S(1)} %slice.46), channel_id=1, source_target_pairs={{3,0},{0,1},{1,2},{2,3},{7,4},{4,5},{5,6},{6,7},{11,8},{8,9},{9,10... | collective-permute-start | bytes 497672 | tf_op jit(solution)/shard_map/ppermute | solution.py:123
  237.2 33.8 %collective-permute-start.3 = (bf16[6,72,6,192]{3,1,2,0:T(8,128)(2,1)S(1)}, bf16[6,72,6,192]{3,1,2,0:T(8,128)(2,1)S(1)}, u32[]{:S(2)}, u32[]{:S(2)}) collective-permute-start(bf16[6,72,6,192]{3,1,2,0:T(8,128)(2,1)S(1)} %copy.28), channel_id=1, source_target_pairs={{124,0},{0,4},{4,8},{8,12},{12,16},{16,20},{20,24},{24,28},{28,32}... | collective-permute-start | bytes 2985992 | tf_op jit(solution)/shard_map/ppermute | solution.py:123
  271.0 5.0 %copy-start.1 = (bf16[2048,256]{1,0:T(8,128)(2,1)S(1)}, bf16[2048,256]{1,0:T(8,128)(2,1)}, u32[]{:S(2)}) copy-start(bf16[2048,256]{1,0:T(8,128)(2,1)} %param.15) | copy-start | bytes 3145732
where the time goes:
time: 277 us; the launch traced here: 276 us
  waiting for transfers between devices  89.2 us (32%)
  Pallas kernels  74.7 us (27%)
  other arithmetic  54 us (19%)
  local copies, waits for them, and re-layouts  34.4 us (12%)
  starting transfers between devices  22.4 us (8%)
    pallas_call x1, Pallas kernels, compute(): pl.pallas_call(kernel, grid=(12,), in_specs=[pl.BlockSpec(memory_space=pl...  74.7 us
    ppermute x4, waiting for transfers between devices, passed_along(): return lax.ppermute(block, axis, route)  60.7 us
    all_to_all x1, waiting for transfers between devices, on_device(): lax.all_to_all(buffer, ('lon', 'lat'), split_axis=0, concat_axis=0, tiled...  28.4 us
    scatter-add x1, other arithmetic, on_device(): obs_field = jnp.zeros((levels * lat_rows * lon_cols, features), jnp.float...  28.1 us
    all_to_all x1, starting transfers between devices, on_device(): lax.all_to_all(cell_ids, ('lon', 'lat'), split_axis=0, concat_axis=0, til...  11.5 us
    scatter x1, local copies, waits for them, and re-layouts, on_device(): buffer = jnp.zeros((devices * capacity, payload.shape[1]), jnp.bfloat16)....  10.9 us
    all_to_all x1, starting transfers between devices, on_device(): lax.all_to_all(buffer, ('lon', 'lat'), split_axis=0, concat_axis=0, tiled...  9.76 us
    convert_element_type x1, other arithmetic, on_device(): (tokens.astype(jnp.float32) + obs_field.reshape(tokens.shape)).astype(jnp...  9.15 us
  transfers between devices with their start and end apart: 6, of which 5 were waited for; matrix products, arithmetic and copies ran while one was open for 9% of the time, Pallas kernels for 0%

commit v1 on v0

--- a/solution.py
+++ b/solution.py
@@ -117,6 +117,108 @@
     )(lat_edge,shifted,bias,g1.reshape(1,D),wq,wp,g2.reshape(1,D),wup,wdn.T)
 
 
+CAP = 32
+DEV = 128
+TN = (((0,), (0,)), ((), ()))
+UN=8
+def pack_kernel(tgt_ref, cell_ref, cnt_ref, val_ref, wt_ref, out_ref, pay, buf):
+    n=val_ref.shape[0]
+    eye=(lax.broadcasted_iota(jnp.int32,(8,64),0)==lax.broadcasted_iota(jnp.int32,(8,64),1)).astype(BF)
+    for c in range(0,n,512):
+        y=lax.dot_general(val_ref[c:c+512,:],wt_ref[...],NT,preferred_element_type=F32)
+        pay[pl.ds(2*c,512,stride=2),:]=y[:,0:128]
+        cell=cell_ref[0:1,c:c+512]
+        ids=jnp.concatenate([(cell>>7).astype(F32),(cell&127).astype(F32),jnp.zeros((6,512),F32)],axis=0).astype(BF)
+        mark=lax.dot_general(ids,eye,TN,preferred_element_type=F32)
+        pay[pl.ds(2*c+1,512,stride=2),:]=jnp.concatenate([y[:,128:192],mark],axis=1)
+    def zero(g,_):
+        buf[pl.ds(pl.multiple_of(g*512,512),512),:]=jnp.zeros((512,128),F32)
+        return 0
+    lax.fori_loop(0,2*DEV*CAP//512,zero,0)
+    count=cnt_ref[0]
+    def body(g,_):
+        for u in range(UN):
+            i=g*UN+u
+            buf[pl.ds(2*tgt_ref[i],2),:]=pay[pl.ds(2*i,2),:]
+        return 0
+    lax.fori_loop(0,(count+UN-1)//UN,body,0)
+    def conv(g,_):
+        r=pl.multiple_of(g*256,256)
+        out_ref[pl.ds(r,256),0:128]=buf[pl.ds(2*r,256,stride=2),:].astype(BF)
+        out_ref[pl.ds(r,256),128:256]=buf[pl.ds(2*r+1,256,stride=2),:].astype(BF)
+        return 0
+    lax.fori_loop(0,DEV*CAP//256,conv,0)
+
+def pack(targets, cells, count, values, w_obs):
+    n=values.shape[0]
+    sm=pl.BlockSpec(memory_space=pltpu.SMEM); vm=pl.BlockSpec(memory_space=pltpu.VMEM)
+    return pl.pallas_call(pack_kernel,in_specs=[sm,vm,sm,vm,vm],out_specs=vm,
+        out_shape=jax.ShapeDtypeStruct((DEV*CAP,256),BF),
+        scratch_shapes=[pltpu.VMEM((2*n,128),F32),pltpu.VMEM((2*DEV*CAP+16,128),F32)],
+        compiler_params=pltpu.CompilerParams(vmem_limit_bytes=40<<20),
+    )(targets,cells.reshape(1,n),count,values,w_obs.T)
+
+NACC=3
+SUN=8
+def scatter_kernel(recv_ref, tok_ref, out_ref, rows, ids_v, ids_s, sem, *accs):
+    cells=tok_ref.shape[0]
+    sel=jnp.where(lax.broadcasted_iota(jnp.int32,(8,256),1)==192,128.0,jnp.where(lax.broadcasted_iota(jnp.int32,(8,256),1)==193,1.0,0.0)).astype(BF)
+    n=recv_ref.shape[0]
+    for c in range(0,n,512):
+        ids=lax.dot_general(sel,recv_ref[c:c+512,:],NT,preferred_element_type=F32)
+        ids_v[0:1,c:c+512]=(ids[0:1]+0.5).astype(jnp.int32)
+    cp=pltpu.make_async_copy(ids_v,ids_s,sem)
+    cp.start()
+    def prep(g,_):
+        r=pl.multiple_of(g*256,256)
+        rows[pl.ds(2*r,256,stride=2),:]=recv_ref[pl.ds(r,256),0:128].astype(F32)
+        rows[pl.ds(2*r+1,256,stride=2),:]=recv_ref[pl.ds(r,256),128:256].astype(F32)
+        return 0
+    lax.fori_loop(0,n//256,prep,0)
+    def init(g,_):
+        r=pl.multiple_of(g*144,144)
+        t=tok_ref[pl.ds(r,144),:].astype(F32)
+        accs[0][pl.ds(2*r,144,stride=2),:]=t[:,0:128]
+        accs[0][pl.ds(2*r+1,144,stride=2),0:64]=t[:,128:192]
+        for a in accs[1:]: a[pl.ds(2*r,288),:]=jnp.zeros((288,128),F32)
+        return 0
+    lax.fori_loop(0,cells//144,init,0)
+    cp.wait()
+    per=n//NACC
+    def body(i,_):
+        for a in range(NACC):
+            j=a*per+i
+            c=ids_s[0,j]
+            accs[a][pl.ds(2*c,2),:]=accs[a][pl.ds(2*c,2),:]+rows[pl.ds(2*j,2),:]
+        return 0
+    lax.fori_loop(0,per,body,0,unroll=SUN)
+    for j in range(per*NACC,n):
+        c=ids_s[0,j]
+        accs[0][pl.ds(2*c,2),:]=accs[0][pl.ds(2*c,2),:]+rows[pl.ds(2*j,2),:]
+    def fin(g,_):
+        r=pl.multiple_of(g*144,144)
+        t=accs[0][pl.ds(2*r,144,stride=2),:]
+        for a in accs[1:]: t=t+a[pl.ds(2*r,144,stride=2),:]
+        out_ref[pl.ds(r,144),0:128]=t.astype(BF)
+        t=accs[0][pl.ds(2*r+1,144,stride=2),:]
+        for a in accs[1:]: t=t+a[pl.ds(2*r+1,144,stride=2),:]
+        out_ref[pl.ds(r,144),128:192]=t[:,0:64].astype(BF)
+        return 0
+    lax.fori_loop(0,cells//144,fin,0)
+
+def scatter(recv, tokens):
+    cells=6*72*24
+    tok=tokens.reshape(cells,D)
+    vm=pl.BlockSpec(memory_space=pltpu.VMEM)
+    n=recv.shape[0]
+    out=pl.pallas_call(scatter_kernel,in_specs=[vm,vm],out_specs=vm,
+        out_shape=jax.ShapeDtypeStruct((cells,D),BF),
+        scratch_shapes=[pltpu.VMEM((2*n,128),F32),pltpu.VMEM((1,n),jnp.int32),pltpu.SMEM((1,n),jnp.int32),pltpu.SemaphoreType.DMA]+[pltpu.VMEM((2*cells,128),F32)]*NACC,
+        compiler_params=pltpu.CompilerParams(vmem_limit_bytes=60<<20),
+    )(recv,tok)
+    return out.reshape(tokens.shape)
+
+
 def passed_along(block, axis, distance):
     devices = range(lax.axis_size(axis))
     route = [((i - distance) % len(devices), i) for i in devices]
@@ -152,23 +254,11 @@
     earlier = jnp.cumsum(matches, axis=0) - matches
     slot_ids = jnp.sum(earlier * matches, axis=1)
     targets = jnp.where(is_live, obs_dest * capacity + slot_ids, devices * capacity)
-    cell_ids = jnp.zeros((devices * capacity,), jnp.int32).at[targets].set(obs_cell, mode="drop")
-    payload = jnp.dot(obs_values, w_obs, preferred_element_type=jnp.float32).astype(jnp.bfloat16)
-    buffer = (
-        jnp.zeros((devices * capacity, payload.shape[1]), jnp.bfloat16)
-        .at[targets]
-        .set(payload, mode="drop")
-    )
-    received, got_cells = (
-        lax.all_to_all(buffer, ("lon", "lat"), split_axis=0, concat_axis=0, tiled=True),
-        lax.all_to_all(cell_ids, ("lon", "lat"), split_axis=0, concat_axis=0, tiled=True),
-    )
-    obs_field = (
-        jnp.zeros((levels * lat_rows * lon_cols, features), jnp.float32)
-        .at[got_cells]
-        .add(received.astype(jnp.float32))
-    )
-    stream = (tokens.astype(jnp.float32) + obs_field.reshape(tokens.shape)).astype(jnp.bfloat16)
+    buffer = pack(targets, obs_cell, obs_count, obs_values, w_obs)
+    received = lax.all_to_all(
+        buffer.reshape(devices, capacity, 256), ("lon", "lat"), split_axis=0, concat_axis=0, tiled=True
+    )
+    stream = scatter(received.reshape(devices * capacity, 256), tokens)
     half_lat = WLAT // 2
     half_lon = WLON // 2
     lat_index = lax.axis_index("lat")

time: 277 us -> 234 us (0.84)
  blocking collectives: 0 us -> 41.9 us
  other arithmetic: 54 us -> 16.8 us
  waiting for transfers between devices: 89.2 us -> 57.1 us
  Pallas kernels: 74.7 us -> 100 us
  starting transfers between devices: 22.4 us -> 1.35 us
  local copies, waits for them, and re-layouts: 34.4 us -> 14.5 us
    all_to_all x0 -> x1, blocking collectives: none -> 41.9 us  [on_device(): lax.all_to_all(buffer.reshape(devices, capacity, 256), ('lon', 'lat'), sp...]
    all_to_all x2 -> x0, waiting for transfers between devices: 28.4 us -> none  [the longest x1 28.4 us: on_device(): lax.all_to_all(buffer, ('lon', 'lat'), split_axis=0, concat_axis=0, tiled...]
    scatter-add x1 -> x0, other arithmetic: 28.1 us -> none  [on_device(): obs_field = jnp.zeros((levels * lat_rows * lon_cols, features), jnp.float...]
    pallas_call x0 -> x2, Pallas kernels: none -> 25.6 us  [the longest x1 20.6 us: scatter(): pl.pallas_call(scatter_kernel, in_specs=[vm, vm], out_specs=vm, out_shape...]
    all_to_all x2 -> x0, starting transfers between devices: 21.2 us -> none  [the longest x1 11.5 us: on_device(): lax.all_to_all(cell_ids, ('lon', 'lat'), split_axis=0, concat_axis=0, til...]
    scatter x2 -> x0, local copies, waits for them, and re-layouts: 19.1 us -> none  [the longest x1 10.9 us: on_device(): buffer = jnp.zeros((devices * capacity, payload.shape[1]), jnp.bfloat16)....]
    convert_element_type x1 -> x0, other arithmetic: 9.15 us -> none  [on_device(): (tokens.astype(jnp.float32) + obs_field.reshape(tokens.shape)).astype(jnp...]
    ppermute x4, waiting for transfers between devices: 60.7 us -> 57.1 us  [passed_along(): return lax.ppermute(block, axis, route)]
  transfers between devices with their start and end apart: 6 -> 4, of which waited for: 5 -> 4; matrix products, arithmetic and copies ran while one was open for 9% -> 7% of each run, Pallas kernels for 0% -> 0%
where the time goes in v1:
time: 234 us; the launch traced here: 233 us
  Pallas kernels  100 us (43%)
  waiting for transfers between devices  57.1 us (24%)
  blocking collectives  41.9 us (18%)
  other arithmetic  16.8 us (7%)
  local copies, waits for them, and re-layouts  14.5 us (6%)
    pallas_call x1, Pallas kernels, compute(): pl.pallas_call(kernel, grid=(12,), in_specs=[pl.BlockSpec(memory_space=pl...  74.7 us
    ppermute x4, waiting for transfers between devices, passed_along(): return lax.ppermute(block, axis, route)  57.1 us
    all_to_all x1, blocking collectives, on_device(): lax.all_to_all(buffer.reshape(devices, capacity, 256), ('lon', 'lat'), sp...  41.9 us
    pallas_call x1, Pallas kernels, scatter(): pl.pallas_call(scatter_kernel, in_specs=[vm, vm], out_specs=vm, out_shape...  20.6 us
    slice x1, local copies, waits for them, and re-layouts, on_device(): widened = jnp.concatenate([stream[:, :, half_lon:], arrived], axis=2)  5.55 us
    pallas_call x1, Pallas kernels, pack(): pl.pallas_call(pack_kernel, in_specs=[sm, vm, sm, vm, vm], out_specs=vm,...  4.94 us
  transfers between devices with their start and end apart: 4, of which 4 were waited for; matrix products, arithmetic and copies ran while one was open for 7% of the time, Pallas kernels for 0%

profile of v1, /device:TPU:1, one launch (start us, length us, event | category | flops | bytes accessed | tf_op | source)
XLA Modules:
  0.0 232.8 jit_solution(2766820961216559342)
XLA Ops:
  0.0 0.0 copy-start.4
  0.0 0.0 copy-start.2
  0.0 0.0 copy-start.1
  0.0 0.0 copy-start
  0.8 0.8 copy.19
  1.6 0.6 fusion.4
  2.2 0.1 broadcast_add_fusion
  2.3 0.3 copy.20
  2.7 0.0 copy-done.4
  2.7 1.1 fusion.3
  3.8 0.0 copy-done.2
  3.9 0.0 copy-done.1
  3.9 0.0 copy-done
  3.9 4.9 %shard_map.136 = bf16[4096,256]{1,0:T(8,128)(2,1)S(1)} custom-call(s32[2048]{0:T(1024)S(1)} %add_select_fusion.tgt_ref, s32[1,2048]{1,0:T(1,128)S(1)} %bitcast.32, s32[1]{0:T(128)} %copy.28.cnt_ref, bf16[2048,256]{1,0:T(8,128)(2,1)S(1)} %copy-done, bf16[192,256]{1,0:T(8,128)(2,1)S(1)} %bitcast.31), custom_call_target="tpu_custom_call" | custom-call | tf_op jit(solution)/shard_map/pallas_call | solution.py:155
  8.8 41.9 %all_to_all.5 = bf16[128,32,256]{2,1,0:T(8,128)(2,1)} all-to-all(bf16[128,32,256]{2,1,0:T(8,128)(2,1)S(1)} %bitcast.30), channel_id=1, replica_groups=mesh['lon'=32,'lat'=4] {'lon','lat'}, dimensions={0} | all-to-all | bytes 4194304 | tf_op jit(solution)/shard_map/all_to_all | solution.py:258
  50.7 20.6 %shard_map.137 = bf16[10368,192]{1,0:T(8,128)(2,1)} custom-call(bf16[4096,256]{1,0:T(8,128)(2,1)} %bitcast.35, bf16[10368,192]{1,0:T(8,128)(2,1)} %bitcast.36), custom_call_target="tpu_custom_call" | custom-call | tf_op jit(solution)/shard_map/pallas_call | solution.py:214
  71.3 0.0 copy-start.3
  71.3 1.6 slice.43
  73.0 0.3 copy.21
  73.3 0.6 collective-permute-start
  73.8 0.0 copy-done.3
  73.8 0.2 copy.23
  74.0 0.9 copy.27.wqkv_ref
  74.9 1.2 broadcast_multiply_fusion
  76.2 3.2 %bitcast_add_fusion.bias_ref = f32[4,864,144]{2,1,0:T(8,128)} fusion(f32[4,144,144]{2,1,0:T(8,128)} %constant.24.clone, f32[864,144]{1,0:T(8,128)S(1)} %bitcast.37), kind=kLoop, calls=%fused_computation.6 | loop fusion | flops 497664 | bytes 2820096 | tf_op jit(solution)/shard_map/add | solution.py:102
  79.4 5.6 %slice.42 = bf16[6,72,18,192]{3,2,1,0:T(8,128)(2,1)S(1)} slice(bf16[6,72,24,192]{3,2,1,0:T(8,128)(2,1)} %bitcast.34), slice={[0:6], [0:72], [6:24], [0:192]} | slice | bytes 5971968 | tf_op jit(solution)/shard_map/slice | solution.py:266
  85.0 18.9 %collective-permute-done = bf16[6,72,6,192]{3,1,2,0:T(8,128)(2,1)S(1)} collective-permute-done((bf16[6,72,6,192]{3,1,2,0:T(8,128)(2,1)S(1)}, bf16[6,72,6,192]{3,1,2,0:T(8,128)(2,1)S(1)}, u32[]{:S(2)}, u32[]{:S(2)}) %collective-permute-start) | collective-permute-done | bytes 995360 | tf_op jit(solution)/shard_map/ppermute | solution.py:225
  103.9 0.3 copy.22
  104.2 0.1 pad_maximum_fusion.3
  104.3 0.6 collective-permute-start.1
  105.0 2.1 fusion.1
  107.1 4.4 %collective-permute-done.1 = bf16[6,3,24,192]{3,2,1,0:T(8,128)(2,1)S(1)} collective-permute-done((bf16[6,3,24,192]{3,2,1,0:T(8,128)(2,1)S(1)}, bf16[6,3,24,192]{3,2,1,0:T(8,128)(2,1)S(1)}, u32[]{:S(2)}, u32[]{:S(2)}) %collective-permute-start.1) | collective-permute-done | bytes 165920 | tf_op jit(solution)/shard_map/ppermute | solution.py:225
  111.4 3.2 %pad_maximum_fusion.1.x_ref = bf16[6,72,24,192]{3,2,1,0:T(8,128)(2,1)} fusion(bf16[6,3,24,192]{3,2,1,0:T(8,128)(2,1)S(1)} %collective-permute-done.1, bf16[6,69,24,192]{3,2,1,0:T(8,128)(2,1)S(1)} %fusion.1), kind=kLoop, calls=%fused_computation.4 | loop fusion | flops 1990656 | bytes 7962624 | tf_op jit(solution)/shard_map/concatenate | solution.py:268
  114.7 74.7 %shard_map.138 = bf16[6,72,24,192]{3,2,1,0:T(8,128)(2,1)} custom-call(s32[1]{0:T(128)} %bitcast.edge_ref, bf16[6,72,24,192]{3,2,1,0:T(8,128)(2,1)} %pad_maximum_fusion.1.x_ref, f32[4,864,144]{2,1,0:T(8,128)} %bitcast_add_fusion.bias_ref, f32[1,192]{1,0:T(1,128)} %bitcast.42, bf16[192,768]{1,0:T(8,128)(2,1)} %copy.27.wqkv_ref, bf16[192,192]{1,0:T(8,128)(2,1)} %wp_ref.1, ...), custom_call_target="tpu_custom_call" | custom-call | tf_op jit(solution)/shard_map/pallas_call | solution.py:108
  189.4 1.0 slice.46
  190.3 0.1 collective-permute-start.2
  190.4 2.8 %slice.47 = bf16[6,69,24,192]{3,2,1,0:T(8,128)(2,1)S(1)} slice(bf16[6,72,24,192]{3,2,1,0:T(8,128)(2,1)} %shard_map.138), slice={[0:6], [0:69], [0:24], [0:192]} | slice | bytes 7630848 | tf_op jit(solution)/shard_map/slice | solution.py:274
  193.2 0.1 collective-permute-done.2
  193.3 0.5 pad_maximum_fusion.2
  193.8 0.3 copy.25
  194.1 0.1 collective-permute-start.3
  194.1 33.7 %collective-permute-done.3 = bf16[6,72,6,192]{3,1,2,0:T(8,128)(2,1)S(1)} collective-permute-done((bf16[6,72,6,192]{3,1,2,0:T(8,128)(2,1)S(1)}, bf16[6,72,6,192]{3,1,2,0:T(8,128)(2,1)S(1)}, u32[]{:S(2)}, u32[]{:S(2)}) %collective-permute-start.3) | collective-permute-done | bytes 995360 | tf_op jit(solution)/shard_map/ppermute | solution.py:225
  227.9 0.4 copy.26
  228.3 4.6 %fusion = bf16[6,72,24,192]{3,2,1,0:T(8,128)(2,1)} fusion(bf16[6,69,24,192]{3,2,1,0:T(8,128)(2,1)S(1)} %slice.47, bf16[6,3,24,192]{3,2,1,0:T(8,128)(2,1)S(1)} %collective-permute-done.2, bf16[6,72,6,192]{3,2,1,0:T(8,128)(2,1)S(1)} %copy.26), kind=kLoop, calls=%fused_computation.1 | loop fusion | flops 11943936 | bytes 8957952 | tf_op jit(solution)/shard_map/concatenate | solution.py:276
  (7 shorter events, 0.1 us)
Async XLA Ops:
  0.0 2.7 %copy-start.4 = (s32[2048]{0:T(1024)S(1)}, s32[2048]{0:T(1024)}, u32[]{:S(2)}) copy-start(s32[2048]{0:T(1024)} %param.16) | copy-start | bytes 24580
  0.0 3.8 %copy-start.2 = (s32[2048]{0:T(1024)S(1)}, s32[2048]{0:T(1024)}, u32[]{:S(2)}) copy-start(s32[2048]{0:T(1024)} %param.17) | copy-start | bytes 24580
  0.0 3.9 %copy-start.1 = (bf16[256,192]{0,1:T(8,128)(2,1)S(1)}, bf16[256,192]{0,1:T(8,128)(2,1)}, u32[]{:S(2)}) copy-start(bf16[256,192]{0,1:T(8,128)(2,1)} %param.19) | copy-start | bytes 294916
  0.0 3.9 %copy-start = (bf16[2048,256]{1,0:T(8,128)(2,1)S(1)}, bf16[2048,256]{1,0:T(8,128)(2,1)}, u32[]{:S(2)}) copy-start(bf16[2048,256]{1,0:T(8,128)(2,1)} %val_ref.1) | copy-start | bytes 3145732
  71.3 2.5 %copy-start.3 = (bf16[192,576]{1,0:T(8,128)(2,1)S(1)}, bf16[192,576]{1,0:T(8,128)(2,1)}, u32[]{:S(2)}) copy-start(bf16[192,576]{1,0:T(8,128)(2,1)} %param.21) | copy-start | bytes 663556
  73.3 30.7 %collective-permute-start = (bf16[6,72,6,192]{3,1,2,0:T(8,128)(2,1)S(1)}, bf16[6,72,6,192]{3,1,2,0:T(8,128)(2,1)S(1)}, u32[]{:S(2)}, u32[]{:S(2)}) collective-permute-start(bf16[6,72,6,192]{3,1,2,0:T(8,128)(2,1)S(1)} %copy.21), channel_id=1, source_target_pairs={{4,0},{8,4},{12,8},{16,12},{20,16},{24,20},{28,24},{32,28},{36,32}... | collective-permute-start | bytes 2985992 | tf_op jit(solution)/shard_map/ppermute | solution.py:225
  104.3 7.1 %collective-permute-start.1 = (bf16[6,3,24,192]{3,2,1,0:T(8,128)(2,1)S(1)}, bf16[6,3,24,192]{3,2,1,0:T(8,128)(2,1)S(1)}, u32[]{:S(2)}, u32[]{:S(2)}) collective-permute-start(bf16[6,3,24,192]{3,2,1,0:T(8,128)(2,1)S(1)} %pad_maximum_fusion.3), channel_id=1, source_target_pairs={{1,0},{2,1},{3,2},{0,3},{5,4},{6,5},{7,6},{4,7},{9,8},{10,9},{11,1... | collective-permute-start | bytes 497672 | tf_op jit(solution)/shard_map/ppermute | solution.py:225
  190.3 3.0 %collective-permute-start.2 = (bf16[6,3,24,192]{3,2,1,0:T(8,128)(2,1)S(1)}, bf16[6,3,24,192]{3,2,1,0:T(8,128)(2,1)S(1)}, u32[]{:S(2)}, u32[]{:S(2)}) collective-permute-start(bf16[6,3,24,192]{3,2,1,0:T(8,128)(2,1)S(1)} %slice.46), channel_id=1, source_target_pairs={{3,0},{0,1},{1,2},{2,3},{7,4},{4,5},{5,6},{6,7},{11,8},{8,9},{9,10... | collective-permute-start | bytes 497672 | tf_op jit(solution)/shard_map/ppermute | solution.py:225
  194.1 33.8 %collective-permute-start.3 = (bf16[6,72,6,192]{3,1,2,0:T(8,128)(2,1)S(1)}, bf16[6,72,6,192]{3,1,2,0:T(8,128)(2,1)S(1)}, u32[]{:S(2)}, u32[]{:S(2)}) collective-permute-start(bf16[6,72,6,192]{3,1,2,0:T(8,128)(2,1)S(1)} %copy.25), channel_id=1, source_target_pairs={{124,0},{0,4},{4,8},{8,12},{12,16},{16,20},{20,24},{24,28},{28,32}... | collective-permute-start | bytes 2985992 | tf_op jit(solution)/shard_map/ppermute | solution.py:225

commit v2 on v1

--- a/solution.py
+++ b/solution.py
@@ -33,63 +33,8 @@
     lane=lax.broadcasted_iota(jnp.int32,shape,len(shape)-1)
     return (lane>=h*width)&(lane<(h+1)*width)
 
-GROUPS=((0,4,0,128),(4,2,128,64))
-
-def kernel(edge_ref, x_ref, bias_ref, g1_ref, wqkv_ref, wp_ref, g2_ref, wup_ref, wdnt_ref, o_ref, xs, s_ref, p_ref, ctx_ref):
-    band=pl.program_id(0)
-    lat_edge=jnp.where(band==pl.num_programs(0)-1, edge_ref[0], 0)
-    zero=jnp.zeros((),BF)
-    def pair(k,_):
-        lvls=(2*k+1, lax.rem(2*k+2,6))
-        for i in range(2):
-            for r in range(6):
-                row=x_ref[lvls[i], r].astype(F32)
-                for w in range(2):
-                    base=w*WIN+(i*6+r)*12
-                    xs[base:base+12,:]=row[w*12:w*12+12]
-        lvl_edge=(k==2).astype(jnp.int32)
-        var=2*lat_edge+lvl_edge
-        n1=norm(xs[...],g1_ref[...])
-        q_all=(dot(n1,wqkv_ref[:,0:256])*np.float32(LOG2E/math.sqrt(HD))).astype(BF)
-        k_all=dot(n1,wqkv_ref[:,256:512]).astype(BF)
-        v_all=dot(n1,wqkv_ref[:,512:768]).astype(BF)
-        for w in range(2):
-            sl=slice(w*WIN,(w+1)*WIN)
-            for h0,nh,l0,ln in GROUPS:
-                qg=q_all[sl,l0:l0+128]; kg=k_all[sl,l0:l0+128]
-                qs=jnp.concatenate([jnp.where(head_mask((WIN,128),h),qg,zero) for h in range(nh)],axis=0)
-                s_ref[w,h0*WIN:(h0+nh)*WIN,:]=dot_nt(qs,kg)
-        for w in range(2):
-            sl=slice(w*WIN,(w+1)*WIN)
-            ls=[]
-            for h in range(HEADS):
-                s=s_ref[w,h*WIN:(h+1)*WIN,:]+bias_ref[var,h*WIN:(h+1)*WIN,:]
-                m=jnp.max(s,axis=-1,keepdims=True)
-                p=jnp.exp2(s-m)
-                ls.append(jnp.sum(p,axis=-1,keepdims=True))
-                p_ref[w,h*WIN:(h+1)*WIN,:]=p.astype(BF)
-            for h0,nh,l0,ln in GROUPS:
-                o=dot(p_ref[w,h0*WIN:(h0+nh)*WIN,:],v_all[sl,l0:l0+128])
-                c=o[:WIN]; l=ls[h0]*jnp.ones((1,128),F32)
-                for h in range(1,nh):
-                    mk=head_mask((WIN,128),h)
-                    c=jnp.where(mk,o[h*WIN:(h+1)*WIN],c)
-                    l=jnp.where(mk,ls[h0+h],l)
-                ctx_ref[sl,l0:l0+128]=(c*(1.0/l)).astype(BF)
-        att=(xs[...]+dot(ctx_ref[:,:D],wp_ref[...])).astype(BF).astype(F32)
-        n2=norm(att,g2_ref[...])
-        acc=att
-        for j in range(3):
-            hid=gelu(dot(n2,wup_ref[:,j*256:(j+1)*256])).astype(BF)
-            acc=acc+dot_nt(hid,wdnt_ref[:,j*256:(j+1)*256])
-        xs[...]=acc
-        for i in range(2):
-            for r in range(6):
-                for w in range(2):
-                    base=w*WIN+(i*6+r)*12
-                    o_ref[lvls[i], r, w*12:w*12+12,:]=xs[base:base+12,:].astype(BF)
-        return 0
-    lax.fori_loop(0,3,pair,0)
+GROUPS=((0,4,0),(4,2,128))
+MESH=pl.DeviceIdType.MESH
 
 def prep_bias(position_bias):
     b=position_bias*np.float32(LOG2E)
@@ -100,21 +45,6 @@
             g=2*le*(row>=3)+ve*lvl
             outs.append((g[:,None]!=g[None,:]).astype(np.float32)*np.float32(-1e30))
     return (b[None]+jnp.asarray(np.stack(outs))[:,None]).reshape(4,HEADS*WIN,WIN)
-
-def compute(shifted, lat_edge, position_bias, g1, wqkv, wp, g2, wup, wdn):
-    bias=prep_bias(position_bias)
-    wq=jnp.pad(wqkv.reshape(D,3,D),((0,0),(0,0),(0,64))).reshape(D,768)
-    full=lambda *s: pl.BlockSpec(s,lambda i:(0,)*len(s),pipeline_mode=pl.Buffered(1))
-    return pl.pallas_call(
-        kernel, grid=(12,),
-        in_specs=[pl.BlockSpec(memory_space=pltpu.SMEM),
-          pl.BlockSpec((6,6,24,D),lambda i:(0,i,0,0)),
-          full(4,HEADS*WIN,WIN),full(1,D),full(D,768),full(D,D),full(1,D),full(D,768),full(D,768)],
-        out_specs=pl.BlockSpec((6,6,24,D),lambda i:(0,i,0,0)),
-        out_shape=jax.ShapeDtypeStruct((6,72,24,D),BF),
-        scratch_shapes=[pltpu.VMEM((2*WIN,D),F32),pltpu.VMEM((2,HEADS*WIN,WIN),F32),pltpu.VMEM((2,HEADS*WIN,WIN),BF),pltpu.VMEM((2*WIN,256),BF)],
-        compiler_params=pltpu.CompilerParams(vmem_limit_bytes=56<<20),
-    )(lat_edge,shifted,bias,g1.reshape(1,D),wq,wp,g2.reshape(1,D),wup,wdn.T)
 
 
 CAP = 32
@@ -219,10 +149,236 @@
     return out.reshape(tokens.shape)
 
 
-def passed_along(block, axis, distance):
-    devices = range(lax.axis_size(axis))
-    route = [((i - distance) % len(devices), i) for i in devices]
-    return lax.ppermute(block, axis, route)
+def attend(xs, s_ref, p_ref, ctx_ref, bias_ref, var, g1_ref, wqkv_ref, wp_ref, g2_ref, wup_ref, wdnt_ref):
+    zero = jnp.zeros((), BF)
+    n1 = norm(xs[...], g1_ref[...])
+    q_all = (dot(n1, wqkv_ref[:, 0:256]) * np.float32(LOG2E / math.sqrt(HD))).astype(BF)
+    k_all = dot(n1, wqkv_ref[:, 256:512]).astype(BF)
+    v_all = dot(n1, wqkv_ref[:, 512:768]).astype(BF)
+    for w in range(2):
+        sl = slice(w * WIN, (w + 1) * WIN)
+        for h0, nh, l0 in GROUPS:
+            qg = q_all[sl, l0 : l0 + 128]
+            kg = k_all[sl, l0 : l0 + 128]
+            qs = jnp.concatenate(
+                [jnp.where(head_mask((WIN, 128), h), qg, zero) for h in range(nh)], axis=0
+            )
+            s_ref[w, h0 * WIN : (h0 + nh) * WIN, :] = dot_nt(qs, kg)
+    for w in range(2):
+        sl = slice(w * WIN, (w + 1) * WIN)
+        sums = []
+        for h in range(HEADS):
+            rows = slice(h * WIN, (h + 1) * WIN)
+            s = s_ref[w, rows, :] + bias_ref[var[w], rows, :]
+            p = jnp.exp2(s - jnp.max(s, axis=-1, keepdims=True))
+            sums.append(jnp.sum(p, axis=-1, keepdims=True))
+            p_ref[w, rows, :] = p.astype(BF)
+        for h0, nh, l0 in GROUPS:
+            o = dot(p_ref[w, h0 * WIN : (h0 + nh) * WIN, :], v_all[sl, l0 : l0 + 128])
+            c = o[:WIN]
+            total = sums[h0] * jnp.ones((1, 128), F32)
+            for h in range(1, nh):
+                mask = head_mask((WIN, 128), h)
+                c = jnp.where(mask, o[h * WIN : (h + 1) * WIN], c)
+                total = jnp.where(mask, sums[h0 + h], total)
+            ctx_ref[sl, l0 : l0 + 128] = (c * (1.0 / total)).astype(BF)
+    att = (xs[...] + dot(ctx_ref[:, :D], wp_ref[...])).astype(BF).astype(F32)
+    n2 = norm(att, g2_ref[...])
+    acc = att
+    for j in range(3):
+        hid = gelu(dot(n2, wup_ref[:, j * 256 : (j + 1) * 256])).astype(BF)
+        acc = acc + dot_nt(hid, wdnt_ref[:, j * 256 : (j + 1) * 256])
+    xs[...] = acc
+
+
+def block_kernel(
+    x_hbm, bias_ref, g1_ref, wqkv_ref, wp_ref, g2_ref, wup_ref, wdnt_ref, o_ref,
+    xe, from_right, from_left, to_right, to_left, back_left, back_right, back_lat, back_diag,
+    xs, s_ref, p_ref, ctx_ref, send_sem, recv_sem, local_sem,
+):
+    lon = lax.axis_index("lon")
+    lat = lax.axis_index("lat")
+    n_lon = lax.axis_size("lon")
+    n_lat = lax.axis_size("lat")
+    east = lax.rem(lon + 1, n_lon)
+    west = lax.rem(lon + n_lon - 1, n_lon)
+    north = lax.rem(lat + 1, n_lat)
+    south = lax.rem(lat + n_lat - 1, n_lat)
+
+    locals_ = [
+        pltpu.make_async_copy(
+            x_hbm.at[:, r0:r1], xe.at[:, r0:r1], local_sem.at[n]
+        )
+        for n, (r0, r1) in enumerate(((0, 39), (39, 72)))
+    ]
+    for copy in locals_:
+        copy.start()
+
+    barrier = pltpu.get_barrier_semaphore()
+    partners = ((east, lat), (west, lat), (lon, north), (lon, south), (east, south), (west, north))
+    for partner in partners:
+        pl.semaphore_signal(barrier, inc=1, device_id=partner, device_id_type=MESH)
+    pl.semaphore_wait(barrier, len(partners))
+
+    def remote(n, src, dst, target):
+        return pltpu.make_async_remote_copy(
+            src_ref=src, dst_ref=dst, send_sem=send_sem.at[n], recv_sem=recv_sem.at[n],
+            device_id=target, device_id_type=MESH,
+        )
+
+    halo = [
+        remote(0, x_hbm.at[:, 3:39, 0:8], from_right, (west, lat)),
+        remote(1, x_hbm.at[:, 39:72, 16:24], from_left.at[:, 0:33], (east, lat)),
+        remote(2, x_hbm.at[:, 0:3], xe.at[:, 72:75], (lon, south)),
+        remote(3, x_hbm.at[:, 0:3, 16:24], from_left.at[:, 33:36], (east, south)),
+    ]
+    home_east = [
+        remote(4 + j, to_right.at[:, 12 * j : 12 * j + 12], back_left.at[:, 12 * j : 12 * j + 12], (east, lat))
+        for j in range(3)
+    ]
+    home_west = [
+        remote(7 + j, to_left.at[:, 12 * j : end], back_right.at[:, 12 * j : end], (west, lat))
+        for j, end in enumerate((12, 24, 33))
+    ]
+    home_diag = remote(10, to_left.at[:, 33:36], back_diag, (west, north))
+    home_lat = remote(11, o_ref.at[:, 72:75], back_lat, (lon, north))
+    for copy in halo:
+        copy.start()
+    locals_[0].wait()
+
+    def step(s, _):
+        phase = s // 9
+        turn = lax.rem(s, 9) // 3
+        k = lax.rem(s, 3)
+        j = jnp.where(phase < 2, turn, 5 - turn)
+        levels = (2 * k + 1, lax.rem(2 * k + 2, 6))
+        inner = (phase == 0) | (phase == 3)
+
+        @pl.when(s == 9)
+        def _():
+            halo[0].wait_recv()
+
+        @pl.when(s == 18)
+        def _():
+            locals_[1].wait()
+            for copy in halo[1:]:
+                copy.wait_recv()
+
+        def places():
+            for i in range(2):
+                for w in range(2):
+                    for r in range(6):
+                        yield levels[i], 3 + 6 * (2 * j + w) + r, w * WIN + (i * 6 + r) * 12
+
+        @pl.when(inner)
+        def _():
+            for level, row, at in places():
+                xs[at : at + 12, :] = xe[level, row].astype(F32)[6:18]
+
+        @pl.when(phase == 1)
+        def _():
+            for level, row, at in places():
+                xs[at : at + 6, :] = xe[level, row, 16:24].astype(F32)[2:8]
+                xs[at + 6 : at + 12, :] = from_right[level, row - 3].astype(F32)[0:6]
+
+        @pl.when(phase == 2)
+        def _():
+            for level, row, at in places():
+                xs[at : at + 6, :] = from_left[level, row - 39].astype(F32)[2:8]
+                xs[at + 6 : at + 12, :] = xe[level, row, 0:8].astype(F32)[0:6]
+
+        lat_edge = ((j == 5) & (lat == n_lat - 1)).astype(jnp.int32)
+        level_edge = (k == 2).astype(jnp.int32)
+        attend(
+            xs, s_ref, p_ref, ctx_ref, bias_ref, (level_edge, 2 * lat_edge + level_edge),
+            g1_ref, wqkv_ref, wp_ref, g2_ref, wup_ref, wdnt_ref,
+        )
+
+        @pl.when(inner)
+        def _():
+            for level, row, at in places():
+                o_ref[level, row, 6:18, :] = xs[at : at + 12, :].astype(BF)
+
+        @pl.when(phase == 1)
+        def _():
+            for level, row, at in places():
+                o_ref[level, row, 18:24, :] = xs[at : at + 6, :].astype(BF)
+                to_right[level, row - 3, 0:6, :] = xs[at + 6 : at + 12, :].astype(BF)
+
+        @pl.when(phase == 2)
+        def _():
+            for level, row, at in places():
+                to_left[level, row - 39, 2:8, :] = xs[at : at + 6, :].astype(BF)
+                o_ref[level, row, 0:6, :] = xs[at + 6 : at + 12, :].astype(BF)
+
+        for n in range(3):
+            @pl.when(s == 11 + 3 * n)
+            def _(n=n):
+                home_east[n].start()
+
+            @pl.when(s == 20 + 3 * n)
+            def _(n=n):
+                home_west[2 - n].start()
+                if n == 0:
+                    home_diag.start()
+
+        @pl.when(s == 29)
+        def _():
+            home_lat.start()
+
+        return 0
+
+    lax.fori_loop(0, 36, step, 0)
+    for copy in home_east:
+        copy.wait_recv()
+    home_lat.wait_recv()
+    home_diag.wait_recv()
+    for copy in home_west:
+        copy.wait_recv()
+
+    def merge(level, _):
+        for r in range(36):
+            o_ref[level, 3 + r, 0:6, :] = back_left[level, r, 0:6, :]
+        for r in range(33):
+            o_ref[level, 39 + r, 18:24, :] = back_right[level, r, 2:8, :]
+        for r in range(3):
+            o_ref[level, r, 0:18, :] = back_lat[level, r, 0:18, :]
+            o_ref[level, r, 18:24, :] = back_diag[level, r, 2:8, :]
+        return 0
+
+    lax.fori_loop(0, 6, merge, 0)
+    for copy in (*halo, *home_east, *home_west, home_diag, home_lat):
+        copy.wait_send()
+
+
+def block(stream, position_bias, g1, wqkv, wp, g2, wup, wdn):
+    bias = prep_bias(position_bias)
+    wq = jnp.pad(wqkv.reshape(D, 3, D), ((0, 0), (0, 0), (0, 64))).reshape(D, 768)
+    vm = pl.BlockSpec(memory_space=pltpu.VMEM)
+    slab = pltpu.VMEM((6, 36, 8, D), BF)
+    out = pl.pallas_call(
+        block_kernel,
+        in_specs=[pl.BlockSpec(memory_space=pl.ANY)] + [vm] * 7,
+        out_specs=vm,
+        out_shape=jax.ShapeDtypeStruct((6, 75, 24, D), BF),
+        scratch_shapes=[
+            pltpu.VMEM((6, 75, 24, D), BF),
+            slab, slab, slab, slab,
+            slab, pltpu.VMEM((6, 33, 8, D), BF),
+            pltpu.VMEM((6, 3, 24, D), BF), pltpu.VMEM((6, 3, 8, D), BF),
+            pltpu.VMEM((2 * WIN, D), F32),
+            pltpu.VMEM((2, HEADS * WIN, WIN), F32),
+            pltpu.VMEM((2, HEADS * WIN, WIN), BF),
+            pltpu.VMEM((2 * WIN, 256), BF),
+            pltpu.SemaphoreType.DMA((12,)),
+            pltpu.SemaphoreType.DMA((12,)),
+            pltpu.SemaphoreType.DMA((2,)),
+        ],
+        compiler_params=pltpu.CompilerParams(
+            collective_id=0, has_side_effects=True, vmem_limit_bytes=56 << 20
+        ),
+    )(stream, bias, g1.reshape(1, D), wq, wp, g2.reshape(1, D), wup, wdn.T)
+    return out[:, :72]
 
 
 def on_device(
@@ -259,21 +415,7 @@
         buffer.reshape(devices, capacity, 256), ("lon", "lat"), split_axis=0, concat_axis=0, tiled=True
     )
     stream = scatter(received.reshape(devices * capacity, 256), tokens)
-    half_lat = WLAT // 2
-    half_lon = WLON // 2
-    lat_index = lax.axis_index("lat")
-    arrived = passed_along(stream[:, :, :half_lon], "lon", -1)
-    widened = jnp.concatenate([stream[:, :, half_lon:], arrived], axis=2)
-    arrived = passed_along(widened[:, :half_lat], "lat", -1)
-    shifted = jnp.concatenate([widened[:, half_lat:], arrived], axis=1)
-    edge = (lat_index == lat_count - 1).astype(jnp.int32).reshape(1)
-    result = compute(
-        shifted, edge, position_bias, ln1_gain, w_qkv, w_proj, ln2_gain, w_up, w_down
-    )
-    arrived = passed_along(result[:, lat_rows - half_lat :], "lat", 1)
-    widened = jnp.concatenate([arrived, result[:, : lat_rows - half_lat]], axis=1)
-    arrived = passed_along(widened[:, :, lon_cols - half_lon :], "lon", 1)
-    return jnp.concatenate([arrived, widened[:, :, : lon_cols - half_lon]], axis=2)
+    return block(stream, position_bias, ln1_gain, w_qkv, w_proj, ln2_gain, w_up, w_down)
 
 
 def solution(mesh):

time: 234 us -> 165 us (0.71)
  blocking collectives: 41.9 us -> 0 us
  waiting for transfers between devices: 57.1 us -> 25.5 us
  Pallas kernels: 100 us -> 113 us
  other arithmetic: 16.8 us -> 5.22 us
  starting transfers between devices: 1.35 us -> 11.5 us
  local copies, waits for them, and re-layouts: 14.5 us -> 8.82 us
    ppermute x4 -> x0, waiting for transfers between devices: 57.1 us -> none  [passed_along(): return lax.ppermute(block, axis, route)]
    all_to_all x1 -> x0, blocking collectives: 41.9 us -> none  [on_device(): lax.all_to_all(buffer.reshape(devices, capacity, 256), ('lon', 'lat'), sp...]
    all_to_all x0 -> x1, waiting for transfers between devices: none -> 25.5 us  [on_device(): lax.all_to_all(buffer.reshape(devices, capacity, 256), ('lon', 'lat'), sp...]
    all_to_all x0 -> x1, starting transfers between devices: none -> 11.5 us  [on_device(): lax.all_to_all(buffer.reshape(devices, capacity, 256), ('lon', 'lat'), sp...]
    pallas_call x1, Pallas kernels: 74.7 us -> 85.6 us  [block(): pl.pallas_call(block_kernel, in_specs=[pl.BlockSpec(memory_space=pl.ANY)]...]
    concatenate x4 -> x0, other arithmetic: 9.97 us -> none  [the longest x1 4.56 us: on_device(): jnp.concatenate([arrived, widened[:, :, :lon_cols - half_lon]], axis=2)]
    slice x6 -> x1, local copies, waits for them, and re-layouts: 11.4 us -> 5.23 us  [block(): return out[:, :72]]
  transfers between devices with their start and end apart: 4 -> 1, of which waited for: 4 -> 1; matrix products, arithmetic and copies ran while one was open for 7% -> 3% of each run, Pallas kernels for 0% -> 0%
where the time goes in v2:
time: 165 us
  Pallas kernels  113 us (68%)
  waiting for transfers between devices  25.5 us (15%)
  starting transfers between devices  11.5 us (7%)
  local copies, waits for them, and re-layouts  8.82 us (5%)
  other arithmetic  5.22 us (3%)
    pallas_call x1, Pallas kernels, block(): pl.pallas_call(block_kernel, in_specs=[pl.BlockSpec(memory_space=pl.ANY)]...  85.6 us
    all_to_all x1, waiting for transfers between devices, on_device(): lax.all_to_all(buffer.reshape(devices, capacity, 256), ('lon', 'lat'), sp...  25.5 us
    pallas_call x1, Pallas kernels, scatter(): pl.pallas_call(scatter_kernel, in_specs=[vm, vm], out_specs=vm, out_shape...  20.6 us
    all_to_all x1, starting transfers between devices, on_device(): lax.all_to_all(buffer.reshape(devices, capacity, 256), ('lon', 'lat'), sp...  11.5 us
    pallas_call x1, Pallas kernels, pack(): pl.pallas_call(pack_kernel, in_specs=[sm, vm, sm, vm, vm], out_specs=vm,...  6.38 us
    slice x1, local copies, waits for them, and re-layouts, block(): return out[:, :72]  5.23 us
  transfers between devices with their start and end apart: 1, of which 1 were waited for; matrix products, arithmetic and copies ran while one was open for 3% of the time, Pallas kernels for 0%

profile of v2, /device:TPU:1, one launch (start us, length us, event | category | flops | bytes accessed | tf_op | source)
XLA Modules:
  0.0 164.6 jit_solution(15549878776117453666)
XLA Ops:
  0.0 0.0 copy-start.6
  0.0 0.0 copy-start.1
  0.0 0.0 copy-start.2
  0.0 0.0 copy-start
  0.8 0.8 copy.15
  1.6 0.6 fusion.2
  2.3 0.1 broadcast_add_fusion
  2.3 0.3 copy.16
  2.7 0.0 copy-done.6
  2.7 1.1 fusion.1
  3.8 0.0 copy-done.1
  3.9 0.0 copy-done.2
  3.9 0.0 copy-done
  3.9 0.0 copy-start.5
  3.9 6.4 %shard_map.136 = bf16[4096,256]{1,0:T(8,128)(2,1)} custom-call(s32[2048]{0:T(1024)S(1)} %add_select_fusion.tgt_ref, s32[1,2048]{1,0:T(1,128)S(1)} %bitcast.30, s32[1]{0:T(128)} %copy.20.cnt_ref, bf16[2048,256]{1,0:T(8,128)(2,1)S(1)} %copy-done, bf16[192,256]{1,0:T(8,128)(2,1)S(1)} %bitcast.29), custom_call_target="tpu_custom_call" | custom-call | tf_op jit(solution)/shard_map/pallas_call | solution.py:85
  10.3 0.0 copy-start.4
  10.3 11.5 %all-to-all-start = ((bf16[128,32,256]{2,1,0:T(8,128)(2,1)}), bf16[128,32,256]{2,1,0:T(8,128)(2,1)S(1)}, u32[]{:S(2)}, u32[]{:S(2)}) async-start(bf16[128,32,256]{2,1,0:T(8,128)(2,1)} %bitcast.7), calls=%async_computation | async-start | bytes 4194304 | tf_op jit(solution)/shard_map/all_to_all | solution.py:414
  21.8 0.0 copy-done.5
  21.8 0.2 copy.17
  22.0 0.9 copy.19.wqkv_ref
  22.9 1.2 broadcast_multiply_fusion
  24.2 0.0 copy-done.4
  24.2 2.1 %bitcast_add_fusion.bias_ref = f32[4,864,144]{2,1,0:T(8,128)} fusion(f32[4,144,144]{2,1,0:T(8,128)S(1)} %copy-done.4, f32[864,144]{1,0:T(8,128)S(1)} %bitcast.34), kind=kLoop, calls=%fused_computation | loop fusion | flops 497664 | bytes 2820096 | tf_op jit(solution)/shard_map/add | solution.py:47
  26.3 25.5 %all-to-all-done = bf16[128,32,256]{2,1,0:T(8,128)(2,1)S(1)} async-done(((bf16[128,32,256]{2,1,0:T(8,128)(2,1)}), bf16[128,32,256]{2,1,0:T(8,128)(2,1)S(1)}, u32[]{:S(2)}, u32[]{:S(2)}) %all-to-all-start) | async-done | bytes 2097184 | tf_op jit(solution)/shard_map/all_to_all | solution.py:414
  51.8 0.0 copy-start.3
  51.8 1.3 copy-done.3
  53.1 20.6 %shard_map.137 = bf16[10368,192]{1,0:T(8,128)(2,1)} custom-call(bf16[4096,256]{1,0:T(8,128)(2,1)} %bitcast.32, bf16[10368,192]{1,0:T(8,128)(2,1)} %bitcast.33), custom_call_target="tpu_custom_call" | custom-call | tf_op jit(solution)/shard_map/pallas_call | solution.py:144
  73.8 85.6 %shard_map.138 = bf16[6,75,24,192]{3,2,1,0:T(8,128)(2,1)} custom-call(bf16[6,72,24,192]{3,2,1,0:T(8,128)(2,1)} %bitcast.31, f32[4,864,144]{2,1,0:T(8,128)} %bitcast_add_fusion.bias_ref, f32[1,192]{1,0:T(1,128)} %bitcast.39, bf16[192,768]{1,0:T(8,128)(2,1)} %copy.19.wqkv_ref, bf16[192,192]{1,0:T(8,128)(2,1)} %wp_ref.1, f32[1,192]{1,0:T(1,128)} %bitcast.40, ...), custom_call_target="tpu_custom_call" | custom-call | tf_op jit(solution)/shard_map/pallas_call | solution.py:359
  159.4 5.2 %slice.11 = bf16[6,72,24,192]{3,2,1,0:T(8,128)(2,1)} slice(bf16[6,75,24,192]{3,2,1,0:T(8,128)(2,1)} %shard_map.138), slice={[0:6], [0:72], [0:24], [0:192]} | slice | bytes 7962624 | tf_op jit(solution)/shard_map/slice | solution.py:381
  (7 shorter events, 0.1 us)
Async XLA Ops:
  0.0 2.7 %copy-start.6 = (s32[2048]{0:T(1024)S(1)}, s32[2048]{0:T(1024)}, u32[]{:S(2)}) copy-start(s32[2048]{0:T(1024)} %param.16) | copy-start | bytes 24580
  0.0 3.8 %copy-start.1 = (bf16[256,192]{0,1:T(8,128)(2,1)S(1)}, bf16[256,192]{0,1:T(8,128)(2,1)}, u32[]{:S(2)}) copy-start(bf16[256,192]{0,1:T(8,128)(2,1)} %param.19) | copy-start | bytes 294916
  0.0 3.9 %copy-start.2 = (s32[2048]{0:T(1024)S(1)}, s32[2048]{0:T(1024)}, u32[]{:S(2)}) copy-start(s32[2048]{0:T(1024)} %param.17) | copy-start | bytes 24580
  0.0 3.9 %copy-start = (bf16[2048,256]{1,0:T(8,128)(2,1)S(1)}, bf16[2048,256]{1,0:T(8,128)(2,1)}, u32[]{:S(2)}) copy-start(bf16[2048,256]{1,0:T(8,128)(2,1)} %val_ref.1) | copy-start | bytes 3145732
  3.9 17.9 %copy-start.5 = (bf16[192,576]{1,0:T(8,128)(2,1)S(1)}, bf16[192,576]{1,0:T(8,128)(2,1)}, u32[]{:S(2)}) copy-start(bf16[192,576]{1,0:T(8,128)(2,1)} %param.21) | copy-start | bytes 663556
  10.3 13.9 %copy-start.4 = (f32[4,144,144]{2,1,0:T(8,128)S(1)}, f32[4,144,144]{2,1,0:T(8,128)}, u32[]{:S(2)}) copy-start(f32[4,144,144]{2,1,0:T(8,128)} %constant.18.clone) | copy-start | bytes 995332
  10.3 41.5 %all-to-all-start = ((bf16[128,32,256]{2,1,0:T(8,128)(2,1)}), bf16[128,32,256]{2,1,0:T(8,128)(2,1)S(1)}, u32[]{:S(2)}, u32[]{:S(2)}) async-start(bf16[128,32,256]{2,1,0:T(8,128)(2,1)} %bitcast.7), calls=%async_computation | async-start | bytes 4194304 | tf_op jit(solution)/shard_map/all_to_all | solution.py:414
  51.8 1.3 copy-start.3

commit v3 on v2

--- a/solution.py
+++ b/solution.py
@@ -85,10 +85,10 @@
     return pl.pallas_call(pack_kernel,in_specs=[sm,vm,sm,vm,vm],out_specs=vm,
         out_shape=jax.ShapeDtypeStruct((DEV*CAP,256),BF),
         scratch_shapes=[pltpu.VMEM((2*n,128),F32),pltpu.VMEM((2*DEV*CAP+16,128),F32)],
-        compiler_params=pltpu.CompilerParams(vmem_limit_bytes=40<<20),
+        compiler_params=pltpu.CompilerParams(vmem_limit_bytes=16<<20),
     )(targets,cells.reshape(1,n),count,values,w_obs.T)
 
-NACC=3
+NACC=2
 SUN=8
 def scatter_kernel(recv_ref, tok_ref, out_ref, rows, ids_v, ids_s, sem, *accs):
     cells=tok_ref.shape[0]
@@ -144,37 +144,42 @@
     out=pl.pallas_call(scatter_kernel,in_specs=[vm,vm],out_specs=vm,
         out_shape=jax.ShapeDtypeStruct((cells,D),BF),
         scratch_shapes=[pltpu.VMEM((2*n,128),F32),pltpu.VMEM((1,n),jnp.int32),pltpu.SMEM((1,n),jnp.int32),pltpu.SemaphoreType.DMA]+[pltpu.VMEM((2*cells,128),F32)]*NACC,
-        compiler_params=pltpu.CompilerParams(vmem_limit_bytes=60<<20),
+        compiler_params=pltpu.CompilerParams(vmem_limit_bytes=30<<20),
     )(recv,tok)
     return out.reshape(tokens.shape)
 
 
-def attend(xs, s_ref, p_ref, ctx_ref, bias_ref, var, g1_ref, wqkv_ref, wp_ref, g2_ref, wup_ref, wdnt_ref):
+def attend(xs, qkv_ref, s_ref, p_ref, ctx_ref, bias_ref, variants, g1_ref, wqkv_ref, wp_ref, g2_ref, wup_ref, wdnt_ref):
     zero = jnp.zeros((), BF)
+    count = len(variants)
     n1 = norm(xs[...], g1_ref[...])
-    q_all = (dot(n1, wqkv_ref[:, 0:256]) * np.float32(LOG2E / math.sqrt(HD))).astype(BF)
-    k_all = dot(n1, wqkv_ref[:, 256:512]).astype(BF)
-    v_all = dot(n1, wqkv_ref[:, 512:768]).astype(BF)
-    for w in range(2):
+    qkv_ref[:, 0:256] = (
+        dot(n1, wqkv_ref[:, 0:256]) * np.float32(LOG2E / math.sqrt(HD))
+    ).astype(BF)
+    qkv_ref[:, 256:512] = dot(n1, wqkv_ref[:, 256:512]).astype(BF)
+    qkv_ref[:, 512:768] = dot(n1, wqkv_ref[:, 512:768]).astype(BF)
+
+    def scores(w):
         sl = slice(w * WIN, (w + 1) * WIN)
         for h0, nh, l0 in GROUPS:
-            qg = q_all[sl, l0 : l0 + 128]
-            kg = k_all[sl, l0 : l0 + 128]
+            qg = qkv_ref[sl, l0 : l0 + 128]
+            kg = qkv_ref[sl, 256 + l0 : 384 + l0]
             qs = jnp.concatenate(
                 [jnp.where(head_mask((WIN, 128), h), qg, zero) for h in range(nh)], axis=0
             )
-            s_ref[w, h0 * WIN : (h0 + nh) * WIN, :] = dot_nt(qs, kg)
-    for w in range(2):
+            s_ref[w % 2, h0 * WIN : (h0 + nh) * WIN, :] = dot_nt(qs, kg)
+
+    def softmax(w):
         sl = slice(w * WIN, (w + 1) * WIN)
         sums = []
         for h in range(HEADS):
             rows = slice(h * WIN, (h + 1) * WIN)
-            s = s_ref[w, rows, :] + bias_ref[var[w], rows, :]
+            s = s_ref[w % 2, rows, :] + bias_ref[variants[w], rows, :]
             p = jnp.exp2(s - jnp.max(s, axis=-1, keepdims=True))
             sums.append(jnp.sum(p, axis=-1, keepdims=True))
-            p_ref[w, rows, :] = p.astype(BF)
+            p_ref[w % 2, rows, :] = p.astype(BF)
         for h0, nh, l0 in GROUPS:
-            o = dot(p_ref[w, h0 * WIN : (h0 + nh) * WIN, :], v_all[sl, l0 : l0 + 128])
+            o = dot(p_ref[w % 2, h0 * WIN : (h0 + nh) * WIN, :], qkv_ref[sl, 512 + l0 : 640 + l0])
             c = o[:WIN]
             total = sums[h0] * jnp.ones((1, 128), F32)
             for h in range(1, nh):
@@ -182,6 +187,12 @@
                 c = jnp.where(mask, o[h * WIN : (h + 1) * WIN], c)
                 total = jnp.where(mask, sums[h0 + h], total)
             ctx_ref[sl, l0 : l0 + 128] = (c * (1.0 / total)).astype(BF)
+
+    scores(0)
+    for w in range(count):
+        if w + 1 < count:
+            scores(w + 1)
+        softmax(w)
     att = (xs[...] + dot(ctx_ref[:, :D], wp_ref[...])).astype(BF).astype(F32)
     n2 = norm(att, g2_ref[...])
     acc = att
@@ -194,7 +205,7 @@
 def block_kernel(
     x_hbm, bias_ref, g1_ref, wqkv_ref, wp_ref, g2_ref, wup_ref, wdnt_ref, o_ref,
     xe, from_right, from_left, to_right, to_left, back_left, back_right, back_lat, back_diag,
-    xs, s_ref, p_ref, ctx_ref, send_sem, recv_sem, local_sem,
+    xs, qkv_ref, s_ref, p_ref, ctx_ref, send_sem, recv_sem, local_sem,
 ):
     lon = lax.axis_index("lon")
     lat = lax.axis_index("lat")
@@ -247,28 +258,27 @@
     locals_[0].wait()
 
     def step(s, _):
-        phase = s // 9
-        turn = lax.rem(s, 9) // 3
-        k = lax.rem(s, 3)
+        phase = s // 3
+        turn = lax.rem(s, 3)
         j = jnp.where(phase < 2, turn, 5 - turn)
-        levels = (2 * k + 1, lax.rem(2 * k + 2, 6))
         inner = (phase == 0) | (phase == 3)
 
-        @pl.when(s == 9)
+        @pl.when(s == 3)
         def _():
             halo[0].wait_recv()
 
-        @pl.when(s == 18)
+        @pl.when(s == 6)
         def _():
             locals_[1].wait()
             for copy in halo[1:]:
                 copy.wait_recv()
 
         def places():
-            for i in range(2):
-                for w in range(2):
+            for w in range(6):
+                for i in range(2):
                     for r in range(6):
-                        yield levels[i], 3 + 6 * (2 * j + w) + r, w * WIN + (i * 6 + r) * 12
+                        level = (w // 2 * 2 + 1 + i) % 6
+                        yield level, 3 + 6 * (2 * j + w % 2) + r, w * WIN + (i * 6 + r) * 12
 
         @pl.when(inner)
         def _():
@@ -288,9 +298,9 @@
                 xs[at + 6 : at + 12, :] = xe[level, row, 0:8].astype(F32)[0:6]
 
         lat_edge = ((j == 5) & (lat == n_lat - 1)).astype(jnp.int32)
-        level_edge = (k == 2).astype(jnp.int32)
+        variants = [w // 4 + (2 * lat_edge if w % 2 else 0) for w in range(6)]
         attend(
-            xs, s_ref, p_ref, ctx_ref, bias_ref, (level_edge, 2 * lat_edge + level_edge),
+            xs, qkv_ref, s_ref, p_ref, ctx_ref, bias_ref, variants,
             g1_ref, wqkv_ref, wp_ref, g2_ref, wup_ref, wdnt_ref,
         )
 
@@ -312,23 +322,23 @@
                 o_ref[level, row, 0:6, :] = xs[at + 6 : at + 12, :].astype(BF)
 
         for n in range(3):
-            @pl.when(s == 11 + 3 * n)
+            @pl.when(s == 3 + n)
             def _(n=n):
                 home_east[n].start()
 
-            @pl.when(s == 20 + 3 * n)
+            @pl.when(s == 6 + n)
             def _(n=n):
                 home_west[2 - n].start()
                 if n == 0:
                     home_diag.start()
 
-        @pl.when(s == 29)
+        @pl.when(s == 9)
         def _():
             home_lat.start()
 
         return 0
 
-    lax.fori_loop(0, 36, step, 0)
+    lax.fori_loop(0, 12, step, 0)
     for copy in home_east:
         copy.wait_recv()
     home_lat.wait_recv()
@@ -366,16 +376,17 @@
             slab, slab, slab, slab,
             slab, pltpu.VMEM((6, 33, 8, D), BF),
             pltpu.VMEM((6, 3, 24, D), BF), pltpu.VMEM((6, 3, 8, D), BF),
-            pltpu.VMEM((2 * WIN, D), F32),
+            pltpu.VMEM((6 * WIN, D), F32),
+            pltpu.VMEM((6 * WIN, 768), BF),
             pltpu.VMEM((2, HEADS * WIN, WIN), F32),
             pltpu.VMEM((2, HEADS * WIN, WIN), BF),
-            pltpu.VMEM((2 * WIN, 256), BF),
+            pltpu.VMEM((6 * WIN, 256), BF),
             pltpu.SemaphoreType.DMA((12,)),
             pltpu.SemaphoreType.DMA((12,)),
             pltpu.SemaphoreType.DMA((2,)),
         ],
         compiler_params=pltpu.CompilerParams(
-            collective_id=0, has_side_effects=True, vmem_limit_bytes=56 << 20
+            collective_id=0, has_side_effects=True, vmem_limit_bytes=34 << 20
         ),
     )(stream, bias, g1.reshape(1, D), wq, wp, g2.reshape(1, D), wup, wdn.T)
     return out[:, :72]

time: 165 us -> 140 us (0.85)
  Pallas kernels: 113 us -> 89.7 us
  other arithmetic: 5.22 us -> 3.36 us
    pallas_call x1, Pallas kernels: 85.6 us -> 65.1 us  [block(): pl.pallas_call(block_kernel, in_specs=[pl.BlockSpec(memory_space=pl.ANY)]...]
    pallas_call x1, Pallas kernels: 20.6 us -> 17.7 us  [scatter(): pl.pallas_call(scatter_kernel, in_specs=[vm, vm], out_specs=vm, out_shape...]
    slice x1, local copies, waits for them, and re-layouts: 5.23 us -> 2.72 us  [block(): return out[:, :72]]
  transfers between devices with their start and end apart: 1 -> 1, of which waited for: 1 -> 1; matrix products, arithmetic and copies ran while one was open for 3% -> 2% of each run, Pallas kernels for 0% -> 0%
where the time goes in v3:
time: 140 us
  Pallas kernels  89.7 us (64%)
  waiting for transfers between devices  27 us (19%)
  starting transfers between devices  11.6 us (8%)
  local copies, waits for them, and re-layouts  7.51 us (5%)
  other arithmetic  3.36 us (2%)
    pallas_call x1, Pallas kernels, block(): pl.pallas_call(block_kernel, in_specs=[pl.BlockSpec(memory_space=pl.ANY)]...  65.1 us
    all_to_all x1, waiting for transfers between devices, on_device(): lax.all_to_all(buffer.reshape(devices, capacity, 256), ('lon', 'lat'), sp...  27 us
    pallas_call x1, Pallas kernels, scatter(): pl.pallas_call(scatter_kernel, in_specs=[vm, vm], out_specs=vm, out_shape...  17.7 us
    all_to_all x1, starting transfers between devices, on_device(): lax.all_to_all(buffer.reshape(devices, capacity, 256), ('lon', 'lat'), sp...  11.6 us
    pallas_call x1, Pallas kernels, pack(): pl.pallas_call(pack_kernel, in_specs=[sm, vm, sm, vm, vm], out_specs=vm,...  6.86 us
  transfers between devices with their start and end apart: 1, of which 1 were waited for; matrix products, arithmetic and copies ran while one was open for 2% of the time, Pallas kernels for 0%

profile of v3, /device:TPU:1, one launch (start us, length us, event | category | flops | bytes accessed | tf_op | source)
XLA Modules:
  0.0 140.1 jit_solution(17473414492579118178)
XLA Ops:
  0.0 0.0 copy-start.12
  0.0 0.0 copy-start.6
  0.0 0.0 copy-start.7
  0.0 0.0 copy-start.2
  0.8 0.8 copy.15
  1.6 0.6 fusion.2
  2.3 0.1 broadcast_add_fusion
  2.3 0.3 copy.16
  2.7 0.0 copy-done.12
  2.7 1.1 fusion.1
  3.8 0.0 copy-done.6
  3.9 0.0 copy-done.7
  3.9 0.0 copy-done.2
  3.9 0.0 copy-start.11
  3.9 6.9 %shard_map.136 = bf16[4096,256]{1,0:T(8,128)(2,1)} custom-call(s32[2048]{0:T(1024)S(1)} %add_select_fusion.tgt_ref, s32[1,2048]{1,0:T(1,128)S(1)} %bitcast.33, s32[1]{0:T(128)} %copy.20.cnt_ref, bf16[2048,256]{1,0:T(8,128)(2,1)S(1)} %copy-done.2, bf16[192,256]{1,0:T(8,128)(2,1)S(1)} %bitcast.32), custom_call_target="tpu_custom_call" | custom-call | tf_op jit(solution)/shard_map/pallas_call | solution.py:85
  10.7 0.0 copy-start.10
  10.7 11.6 %all-to-all-start = ((bf16[128,32,256]{2,1,0:T(8,128)(2,1)}), bf16[128,32,256]{2,1,0:T(8,128)(2,1)}, u32[]{:S(2)}, u32[]{:S(2)}) async-start(bf16[128,32,256]{2,1,0:T(8,128)(2,1)} %bitcast.7), calls=%async_computation | async-start | bytes 4194304 | tf_op jit(solution)/shard_map/all_to_all | solution.py:425
  22.3 0.0 copy-done.11
  22.3 0.2 copy.17
  22.6 0.9 copy.19.wqkv_ref
  23.4 0.0 copy-done.10
  23.4 0.1 broadcast_multiply_fusion
  23.5 1.4 bitcast_add_fusion.bias_ref
  24.9 27.0 %all-to-all-done = bf16[128,32,256]{2,1,0:T(8,128)(2,1)} async-done(((bf16[128,32,256]{2,1,0:T(8,128)(2,1)}), bf16[128,32,256]{2,1,0:T(8,128)(2,1)}, u32[]{:S(2)}, u32[]{:S(2)}) %all-to-all-start) | async-done | bytes 2097184 | tf_op jit(solution)/shard_map/all_to_all | solution.py:425
  52.0 0.0 copy-start
  52.0 2.5 %copy-done = bf16[6,72,24,192]{3,2,1,0:T(8,128)(2,1)S(1)} copy-done((bf16[6,72,24,192]{3,2,1,0:T(8,128)(2,1)S(1)}, bf16[6,72,24,192]{3,2,1,0:T(8,128)(2,1)}, u32[]{:S(2)}) %copy-start) | copy-done | bytes 3981336
  54.5 0.0 copy-start.1
  54.5 0.0 copy-start.3
  54.5 0.0 copy-start.4
  54.5 0.0 copy-start.5
  54.5 0.0 copy-start.8
  54.5 0.0 copy-start.9
  54.5 17.7 %shard_map.137 = bf16[10368,192]{1,0:T(8,128)(2,1)S(1)} custom-call(bf16[4096,256]{1,0:T(8,128)(2,1)} %bitcast.8.recv_ref, bf16[10368,192]{1,0:T(8,128)(2,1)S(1)} %bitcast.30), custom_call_target="tpu_custom_call" | custom-call | tf_op jit(solution)/shard_map/pallas_call | solution.py:144
  72.2 0.0 copy-done.1
  72.2 0.0 copy-done.3
  72.2 0.0 copy-done.4
  72.3 0.0 copy-done.5
  72.3 0.0 copy-done.8
  72.3 0.0 copy-done.9
  72.3 65.1 %shard_map.138 = bf16[6,75,24,192]{3,2,1,0:T(8,128)(2,1)S(1)} custom-call(bf16[6,72,24,192]{3,2,1,0:T(8,128)(2,1)S(1)} %bitcast.29, f32[4,864,144]{2,1,0:T(8,128)S(1)} %bitcast_add_fusion.bias_ref, f32[1,192]{1,0:T(1,128)S(1)} %bitcast.34, bf16[192,768]{1,0:T(8,128)(2,1)S(1)} %copy-done.1, bf16[192,192]{1,0:T(8,128)(2,1)S(1)} %copy-done.5, ...), custom_call_target="tpu_custom_call" | custom-call | tf_op jit(solution)/shard_map/pallas_call | solution.py:369
  137.4 2.7 %slice.11 = bf16[6,72,24,192]{3,2,1,0:T(8,128)(2,1)} slice(bf16[6,75,24,192]{3,2,1,0:T(8,128)(2,1)S(1)} %shard_map.138), slice={[0:6], [0:72], [0:24], [0:192]} | slice | bytes 7962624 | tf_op jit(solution)/shard_map/slice | solution.py:392
  (7 shorter events, 0.1 us)
Async XLA Ops:
  0.0 2.7 %copy-start.12 = (s32[2048]{0:T(1024)S(1)}, s32[2048]{0:T(1024)}, u32[]{:S(2)}) copy-start(s32[2048]{0:T(1024)} %param.16) | copy-start | bytes 24580
  0.0 3.8 %copy-start.6 = (bf16[256,192]{0,1:T(8,128)(2,1)S(1)}, bf16[256,192]{0,1:T(8,128)(2,1)}, u32[]{:S(2)}) copy-start(bf16[256,192]{0,1:T(8,128)(2,1)} %param.19) | copy-start | bytes 294916
  0.0 3.9 %copy-start.7 = (s32[2048]{0:T(1024)S(1)}, s32[2048]{0:T(1024)}, u32[]{:S(2)}) copy-start(s32[2048]{0:T(1024)} %param.17) | copy-start | bytes 24580
  0.0 3.9 %copy-start.2 = (bf16[2048,256]{1,0:T(8,128)(2,1)S(1)}, bf16[2048,256]{1,0:T(8,128)(2,1)}, u32[]{:S(2)}) copy-start(bf16[2048,256]{1,0:T(8,128)(2,1)} %val_ref.1) | copy-start | bytes 3145732
  3.9 18.5 %copy-start.11 = (bf16[192,576]{1,0:T(8,128)(2,1)S(1)}, bf16[192,576]{1,0:T(8,128)(2,1)}, u32[]{:S(2)}) copy-start(bf16[192,576]{1,0:T(8,128)(2,1)} %param.21) | copy-start | bytes 663556
  10.7 12.7 %copy-start.10 = (f32[6,144,144]{2,1,0:T(8,128)S(1)}, f32[6,144,144]{2,1,0:T(8,128)}, u32[]{:S(2)}) copy-start(f32[6,144,144]{2,1,0:T(8,128)} %param.22) | copy-start | bytes 1492996
  10.7 41.2 %all-to-all-start = ((bf16[128,32,256]{2,1,0:T(8,128)(2,1)}), bf16[128,32,256]{2,1,0:T(8,128)(2,1)}, u32[]{:S(2)}, u32[]{:S(2)}) async-start(bf16[128,32,256]{2,1,0:T(8,128)(2,1)} %bitcast.7), calls=%async_computation | async-start | bytes 4194304 | tf_op jit(solution)/shard_map/all_to_all | solution.py:425
  52.0 2.5 %copy-start = (bf16[6,72,24,192]{3,2,1,0:T(8,128)(2,1)S(1)}, bf16[6,72,24,192]{3,2,1,0:T(8,128)(2,1)}, u32[]{:S(2)}) copy-start(bf16[6,72,24,192]{3,2,1,0:T(8,128)(2,1)} %param.14) | copy-start | bytes 11943940
  54.5 17.8 %copy-start.1 = (bf16[192,768]{1,0:T(8,128)(2,1)S(1)}, bf16[192,768]{1,0:T(8,128)(2,1)}, u32[]{:S(2)}) copy-start(bf16[192,768]{1,0:T(8,128)(2,1)} %copy.19.wqkv_ref) | copy-start | bytes 884740
  54.5 17.8 %copy-start.3 = (bf16[192,768]{1,0:T(8,128)(2,1)S(1)}, bf16[192,768]{1,0:T(8,128)(2,1)}, u32[]{:S(2)}) copy-start(bf16[192,768]{1,0:T(8,128)(2,1)} %wup_ref.1) | copy-start | bytes 884740
  54.5 17.8 %copy-start.4 = (bf16[768,192]{0,1:T(8,128)(2,1)S(1)}, bf16[768,192]{0,1:T(8,128)(2,1)}, u32[]{:S(2)}) copy-start(bf16[768,192]{0,1:T(8,128)(2,1)} %param.26) | copy-start | bytes 884740
  54.5 17.8 %copy-start.5 = (bf16[192,192]{1,0:T(8,128)(2,1)S(1)}, bf16[192,192]{1,0:T(8,128)(2,1)}, u32[]{:S(2)}) copy-start(bf16[192,192]{1,0:T(8,128)(2,1)} %wp_ref.1) | copy-start | bytes 221188
  54.5 17.8 %copy-start.8 = (f32[192]{0:T(256)S(1)}, f32[192]{0:T(256)}, u32[]{:S(2)}) copy-start(f32[192]{0:T(256)} %param.20) | copy-start | bytes 2308
  54.5 17.8 %copy-start.9 = (f32[192]{0:T(256)S(1)}, f32[192]{0:T(256)}, u32[]{:S(2)}) copy-start(f32[192]{0:T(256)} %param.24) | copy-start | bytes 2308

commit v4 on v3

--- a/solution.py
+++ b/solution.py
@@ -49,103 +49,241 @@
 
 CAP = 32
 DEV = 128
+BLK = 56
+CHUNK = 32
 TN = (((0,), (0,)), ((), ()))
-UN=8
-def pack_kernel(tgt_ref, cell_ref, cnt_ref, val_ref, wt_ref, out_ref, pay, buf):
-    n=val_ref.shape[0]
-    eye=(lax.broadcasted_iota(jnp.int32,(8,64),0)==lax.broadcasted_iota(jnp.int32,(8,64),1)).astype(BF)
-    for c in range(0,n,512):
-        y=lax.dot_general(val_ref[c:c+512,:],wt_ref[...],NT,preferred_element_type=F32)
-        pay[pl.ds(2*c,512,stride=2),:]=y[:,0:128]
-        cell=cell_ref[0:1,c:c+512]
-        ids=jnp.concatenate([(cell>>7).astype(F32),(cell&127).astype(F32),jnp.zeros((6,512),F32)],axis=0).astype(BF)
-        mark=lax.dot_general(ids,eye,TN,preferred_element_type=F32)
-        pay[pl.ds(2*c+1,512,stride=2),:]=jnp.concatenate([y[:,128:192],mark],axis=1)
-    def zero(g,_):
-        buf[pl.ds(pl.multiple_of(g*512,512),512),:]=jnp.zeros((512,128),F32)
-        return 0
-    lax.fori_loop(0,2*DEV*CAP//512,zero,0)
-    count=cnt_ref[0]
-    def body(g,_):
-        for u in range(UN):
-            i=g*UN+u
-            buf[pl.ds(2*tgt_ref[i],2),:]=pay[pl.ds(2*i,2),:]
-        return 0
-    lax.fori_loop(0,(count+UN-1)//UN,body,0)
-    def conv(g,_):
-        r=pl.multiple_of(g*256,256)
-        out_ref[pl.ds(r,256),0:128]=buf[pl.ds(2*r,256,stride=2),:].astype(BF)
-        out_ref[pl.ds(r,256),128:256]=buf[pl.ds(2*r+1,256,stride=2),:].astype(BF)
-        return 0
-    lax.fori_loop(0,DEV*CAP//256,conv,0)
-
-def pack(targets, cells, count, values, w_obs):
-    n=values.shape[0]
-    sm=pl.BlockSpec(memory_space=pltpu.SMEM); vm=pl.BlockSpec(memory_space=pltpu.VMEM)
-    return pl.pallas_call(pack_kernel,in_specs=[sm,vm,sm,vm,vm],out_specs=vm,
-        out_shape=jax.ShapeDtypeStruct((DEV*CAP,256),BF),
-        scratch_shapes=[pltpu.VMEM((2*n,128),F32),pltpu.VMEM((2*DEV*CAP+16,128),F32)],
-        compiler_params=pltpu.CompilerParams(vmem_limit_bytes=16<<20),
-    )(targets,cells.reshape(1,n),count,values,w_obs.T)
-
-NACC=2
-SUN=8
+
+
+def ship_kernel(
+    cnt_ref, dest_ref, cell_ref, val_ref, wt_ref, o_ref, y_ref, slot_ref, acc_ref, buf_ref,
+    send_sem, recv_sem, local_sem,
+):
+    n_lat = lax.axis_size("lat")
+    n = lax.axis_size("lon") * n_lat
+    me = lax.axis_index("lon") * n_lat + lax.axis_index("lat")
+    rows = val_ref.shape[0]
+
+    def at(device):
+        return (device // n_lat, lax.rem(device, n_lat))
+
+    barrier = pltpu.get_barrier_semaphore()
+
+    def greet(i, _):
+        pl.semaphore_signal(
+            barrier, inc=1, device_id=at(lax.rem(me + i, n)), device_id_type=MESH
+        )
+        return 0
+
+    lax.fori_loop(1, n, greet, 0)
+
+    eye = (
+        lax.broadcasted_iota(jnp.int32, (8, 64), 0) == lax.broadcasted_iota(jnp.int32, (8, 64), 1)
+    ).astype(BF)
+    for c in range(0, rows, 512):
+        y = dot_nt(val_ref[c : c + 512, :], wt_ref[...])
+        cell = cell_ref[0:1, c : c + 512]
+        ids = jnp.concatenate(
+            [(cell >> 7).astype(F32), (cell & 127).astype(F32), jnp.zeros((6, 512), F32)], axis=0
+        ).astype(BF)
+        mark = lax.dot_general(ids, eye, TN, preferred_element_type=F32)
+        y_ref[c : c + 512, 0:128] = y[:, 0:128].astype(BF)
+        y_ref[c : c + 512, 128:256] = jnp.concatenate([y[:, 128:192], mark], axis=1).astype(BF)
+
+    ahead = (
+        lax.broadcasted_iota(jnp.int32, (256, 256), 0)
+        < lax.broadcasted_iota(jnp.int32, (256, 256), 1)
+    ).astype(F32).astype(BF)
+    tile = lax.broadcasted_iota(jnp.int32, (DEV, 256), 0)
+    carry = jnp.zeros((DEV, 1), F32)
+    for c in range(0, rows, 256):
+        dest = dest_ref[0:1, c : c + 256]
+        live = lax.broadcasted_iota(jnp.int32, (1, 256), 1) + c < cnt_ref[0]
+        away = dest - me + jnp.where(dest < me, n, 0)
+        away = jnp.where(live, away, -1)
+        match = (tile == away).astype(F32)
+        before = dot(match.astype(BF), ahead) + carry
+        rank = jnp.sum(match * before, axis=0, keepdims=True)
+        carry = carry + jnp.sum(match, axis=1, keepdims=True)
+        slot_ref[0:1, c : c + 256] = jnp.where(live, away * CAP + rank.astype(jnp.int32), -1)
+
+    def copy_to(i):
+        return pltpu.make_async_remote_copy(
+            src_ref=buf_ref.at[i], dst_ref=o_ref.at[me],
+            send_sem=send_sem.at[i], recv_sem=recv_sem.at[i],
+            device_id=at(lax.rem(me + i, n)), device_id_type=MESH,
+        )
+
+    def copy_from(i):
+        source = lax.rem(me + n - i, n)
+        return pltpu.make_async_remote_copy(
+            src_ref=buf_ref.at[i], dst_ref=o_ref.at[source],
+            send_sem=send_sem.at[i], recv_sem=recv_sem.at[i],
+            device_id=at(source), device_id_type=MESH,
+        )
+
+    lane = lax.broadcasted_iota(jnp.int32, (16, 128), 1)
+    span = CHUNK * CAP
+    index = lax.broadcasted_iota(jnp.int32, (span, 256), 0)
+
+    def chunk(c, _):
+        for b in range(0, rows, 256):
+            hot = (index == slot_ref[0:1, b : b + 256] - c * span).astype(F32).astype(BF)
+            part = dot(hot, y_ref[b : b + 256, :])
+            if b == 0:
+                acc_ref[...] = part
+            else:
+                acc_ref[...] += part
+
+        def lay(i, _):
+            r = pl.multiple_of(i * CAP, CAP)
+            block = c * CHUNK + i
+            buf_ref[block, 0:32, :] = acc_ref[pl.ds(r, 32), 0:128].astype(BF)
+            rest = acc_ref[pl.ds(r, 32), 128:256]
+            buf_ref[block, 32:48, :] = jnp.where(
+                lane < 64, rest[0:16], pltpu.roll(rest[16:32], 64, 1)
+            ).astype(BF)
+            marks = jnp.zeros((8, 128), F32)
+            for g in range(4):
+                marks = jnp.where(
+                    lane[:8] // 2 == g, pltpu.roll(rest[8 * g : 8 * g + 8], 64 + 2 * g, 1), marks
+                )
+            buf_ref[block, 48:56, :] = marks.astype(BF)
+            return 0
+
+        lax.fori_loop(0, CHUNK, lay, 0, unroll=4)
+
+        @pl.when(c == 0)
+        def _():
+            pl.semaphore_wait(barrier, n - 1)
+
+        def send(i, _):
+            copy_to(c * CHUNK + i).start()
+            return 0
+
+        lax.fori_loop(jnp.where(c == 0, 1, 0), CHUNK, send, 0)
+        return 0
+
+    lax.fori_loop(0, DEV // CHUNK, chunk, 0)
+    local = pltpu.make_async_copy(buf_ref.at[0], o_ref.at[me], local_sem)
+    local.start()
+
+    def land(i, _):
+        copy_from(i).wait_recv()
+        return 0
+
+    lax.fori_loop(1, n, land, 0)
+
+    def sent(i, _):
+        copy_to(i).wait_send()
+        return 0
+
+    lax.fori_loop(1, n, sent, 0)
+    local.wait()
+
+
+def ship(obs_dest, obs_cell, obs_count, values, w_obs):
+    rows = values.shape[0]
+    sm = pl.BlockSpec(memory_space=pltpu.SMEM)
+    vm = pl.BlockSpec(memory_space=pltpu.VMEM)
+    return pl.pallas_call(
+        ship_kernel,
+        in_specs=[sm, vm, vm, vm, vm],
+        out_specs=vm,
+        out_shape=jax.ShapeDtypeStruct((DEV, BLK, 128), BF),
+        scratch_shapes=[
+            pltpu.VMEM((rows, 256), BF),
+            pltpu.VMEM((1, rows), jnp.int32),
+            pltpu.VMEM((CHUNK * CAP, 256), F32),
+            pltpu.VMEM((DEV, BLK, 128), BF),
+            pltpu.SemaphoreType.DMA((DEV,)),
+            pltpu.SemaphoreType.DMA((DEV,)),
+            pltpu.SemaphoreType.DMA,
+        ],
+        compiler_params=pltpu.CompilerParams(
+            collective_id=1, has_side_effects=True, vmem_limit_bytes=20 << 20
+        ),
+    )(obs_count, obs_dest.reshape(1, rows), obs_cell.reshape(1, rows), values, w_obs.T)
+
+
 def scatter_kernel(recv_ref, tok_ref, out_ref, rows, ids_v, ids_s, sem, *accs):
-    cells=tok_ref.shape[0]
-    sel=jnp.where(lax.broadcasted_iota(jnp.int32,(8,256),1)==192,128.0,jnp.where(lax.broadcasted_iota(jnp.int32,(8,256),1)==193,1.0,0.0)).astype(BF)
-    n=recv_ref.shape[0]
-    for c in range(0,n,512):
-        ids=lax.dot_general(sel,recv_ref[c:c+512,:],NT,preferred_element_type=F32)
-        ids_v[0:1,c:c+512]=(ids[0:1]+0.5).astype(jnp.int32)
-    cp=pltpu.make_async_copy(ids_v,ids_s,sem)
+    cells = tok_ref.shape[0]
+    group = lax.broadcasted_iota(jnp.int32, (8, 128), 0)
+    lane = lax.broadcasted_iota(jnp.int32, (8, 128), 1)
+    sel = jnp.where(lane == 2 * group, 128.0, jnp.where(lane == 2 * group + 1, 1.0, 0.0)).astype(BF)
+    for b in range(8):
+        marks = recv_ref[16 * b : 16 * b + 16, 48:56, :].astype(F32).reshape(128, 128).astype(BF)
+        ids_v[:, 128 * b : 128 * b + 128] = (dot_nt(sel, marks) + 0.5).astype(jnp.int32)
+    cp = pltpu.make_async_copy(ids_v, ids_s, sem)
     cp.start()
-    def prep(g,_):
-        r=pl.multiple_of(g*256,256)
-        rows[pl.ds(2*r,256,stride=2),:]=recv_ref[pl.ds(r,256),0:128].astype(F32)
-        rows[pl.ds(2*r+1,256,stride=2),:]=recv_ref[pl.ds(r,256),128:256].astype(F32)
-        return 0
-    lax.fori_loop(0,n//256,prep,0)
-    def init(g,_):
-        r=pl.multiple_of(g*144,144)
-        t=tok_ref[pl.ds(r,144),:].astype(F32)
-        accs[0][pl.ds(2*r,144,stride=2),:]=t[:,0:128]
-        accs[0][pl.ds(2*r+1,144,stride=2),0:64]=t[:,128:192]
-        for a in accs[1:]: a[pl.ds(2*r,288),:]=jnp.zeros((288,128),F32)
-        return 0
-    lax.fori_loop(0,cells//144,init,0)
+
+    def prep(d, _):
+        r = pl.multiple_of(d * 64, 64)
+        rows[pl.ds(r, 32, stride=2), :] = recv_ref[d, 0:32, :].astype(F32)
+        rest = recv_ref[d, 32:48, :].astype(F32)
+        rows[pl.ds(r + 1, 16, stride=2), :] = rest
+        rows[pl.ds(r + 33, 16, stride=2), :] = pltpu.roll(rest, 64, 1)
+        return 0
+
+    lax.fori_loop(0, DEV, prep, 0, unroll=4)
+
+    def init(g, _):
+        r = pl.multiple_of(g * 144, 144)
+        t = tok_ref[pl.ds(r, 144), :].astype(F32)
+        accs[0][pl.ds(2 * r, 144, stride=2), :] = t[:, 0:128]
+        accs[0][pl.ds(2 * r + 1, 144, stride=2), 0:64] = t[:, 128:192]
+        for a in accs[1:]:
+            a[pl.ds(2 * r, 288), :] = jnp.zeros((288, 128), F32)
+        return 0
+
+    lax.fori_loop(0, cells // 144, init, 0)
     cp.wait()
-    per=n//NACC
-    def body(i,_):
-        for a in range(NACC):
-            j=a*per+i
-            c=ids_s[0,j]
-            accs[a][pl.ds(2*c,2),:]=accs[a][pl.ds(2*c,2),:]+rows[pl.ds(2*j,2),:]
-        return 0
-    lax.fori_loop(0,per,body,0,unroll=SUN)
-    for j in range(per*NACC,n):
-        c=ids_s[0,j]
-        accs[0][pl.ds(2*c,2),:]=accs[0][pl.ds(2*c,2),:]+rows[pl.ds(2*j,2),:]
-    def fin(g,_):
-        r=pl.multiple_of(g*144,144)
-        t=accs[0][pl.ds(2*r,144,stride=2),:]
-        for a in accs[1:]: t=t+a[pl.ds(2*r,144,stride=2),:]
-        out_ref[pl.ds(r,144),0:128]=t.astype(BF)
-        t=accs[0][pl.ds(2*r+1,144,stride=2),:]
-        for a in accs[1:]: t=t+a[pl.ds(2*r+1,144,stride=2),:]
-        out_ref[pl.ds(r,144),128:192]=t[:,0:64].astype(BF)
-        return 0
-    lax.fori_loop(0,cells//144,fin,0)
+    half = DEV // len(accs)
+
+    def body(d, _):
+        for j in range(CAP):
+            for a, acc in enumerate(accs):
+                src = d + a * half
+                c = ids_s[j // 8, src * 8 + j % 8]
+                acc[pl.ds(2 * c, 2), :] = (
+                    acc[pl.ds(2 * c, 2), :] + rows[pl.ds(2 * (src * CAP + j), 2), :]
+                )
+        return 0
+
+    lax.fori_loop(0, half, body, 0)
+
+    def fin(g, _):
+        r = pl.multiple_of(g * 144, 144)
+        t = accs[0][pl.ds(2 * r, 144, stride=2), :]
+        for a in accs[1:]:
+            t = t + a[pl.ds(2 * r, 144, stride=2), :]
+        out_ref[pl.ds(r, 144), 0:128] = t.astype(BF)
+        t = accs[0][pl.ds(2 * r + 1, 144, stride=2), :]
+        for a in accs[1:]:
+            t = t + a[pl.ds(2 * r + 1, 144, stride=2), :]
+        out_ref[pl.ds(r, 144), 128:192] = t[:, 0:64].astype(BF)
+        return 0
+
+    lax.fori_loop(0, cells // 144, fin, 0)
+
 
 def scatter(recv, tokens):
-    cells=6*72*24
-    tok=tokens.reshape(cells,D)
-    vm=pl.BlockSpec(memory_space=pltpu.VMEM)
-    n=recv.shape[0]
-    out=pl.pallas_call(scatter_kernel,in_specs=[vm,vm],out_specs=vm,
-        out_shape=jax.ShapeDtypeStruct((cells,D),BF),
-        scratch_shapes=[pltpu.VMEM((2*n,128),F32),pltpu.VMEM((1,n),jnp.int32),pltpu.SMEM((1,n),jnp.int32),pltpu.SemaphoreType.DMA]+[pltpu.VMEM((2*cells,128),F32)]*NACC,
-        compiler_params=pltpu.CompilerParams(vmem_limit_bytes=30<<20),
-    )(recv,tok)
+    cells = 6 * 72 * 24
+    vm = pl.BlockSpec(memory_space=pltpu.VMEM)
+    out = pl.pallas_call(
+        scatter_kernel,
+        in_specs=[vm, vm],
+        out_specs=vm,
+        out_shape=jax.ShapeDtypeStruct((cells, D), BF),
+        scratch_shapes=[
+            pltpu.VMEM((2 * DEV * CAP, 128), F32),
+            pltpu.VMEM((8, 1024), jnp.int32),
+            pltpu.SMEM((8, 1024), jnp.int32),
+            pltpu.SemaphoreType.DMA,
+            pltpu.VMEM((2 * cells, 128), F32),
+            pltpu.VMEM((2 * cells, 128), F32),
+        ],
+        compiler_params=pltpu.CompilerParams(vmem_limit_bytes=30 << 20),
+    )(recv, tokens.reshape(cells, D))
     return out.reshape(tokens.shape)
 
 
@@ -407,25 +545,8 @@
     w_up,
     w_down,
 ):
-    levels, lat_rows, lon_cols, features = tokens.shape
-    lon_count = lax.axis_size("lon")
-    lat_count = lax.axis_size("lat")
-    devices = lon_count * lat_count
-    row_count = obs_values.shape[0]
-    capacity = 2 * row_count // devices
-    position = jnp.arange(row_count, dtype=jnp.int32)
-    is_live = position < obs_count[0]
-    matches = (
-        (obs_dest[:, None] == jnp.arange(devices, dtype=jnp.int32)[None, :]) & is_live[:, None]
-    ).astype(jnp.int32)
-    earlier = jnp.cumsum(matches, axis=0) - matches
-    slot_ids = jnp.sum(earlier * matches, axis=1)
-    targets = jnp.where(is_live, obs_dest * capacity + slot_ids, devices * capacity)
-    buffer = pack(targets, obs_cell, obs_count, obs_values, w_obs)
-    received = lax.all_to_all(
-        buffer.reshape(devices, capacity, 256), ("lon", "lat"), split_axis=0, concat_axis=0, tiled=True
-    )
-    stream = scatter(received.reshape(devices * capacity, 256), tokens)
+    received = ship(obs_dest, obs_cell, obs_count, obs_values, w_obs)
+    stream = scatter(received, tokens)
     return block(stream, position_bias, ln1_gain, w_qkv, w_proj, ln2_gain, w_up, w_down)
 
 

time: 140 us -> 132 us (0.943)
  Pallas kernels: 89.7 us -> 124 us
  waiting for transfers between devices: 27 us -> 0 us
  starting transfers between devices: 11.6 us -> 0 us
  local copies, waits for them, and re-layouts: 7.51 us -> 4.09 us
  other arithmetic: 3.36 us -> 1.67 us
    pallas_call x1, Pallas kernels: 6.86 us -> 40.1 us  [ship(): pl.pallas_call(ship_kernel, in_specs=[sm, vm, vm, vm, vm], out_specs=vm,...]
    all_to_all x1 -> x0, waiting for transfers between devices: 27 us -> none  [on_device(): lax.all_to_all(buffer.reshape(devices, capacity, 256), ('lon', 'lat'), sp...]
    all_to_all x1 -> x0, starting transfers between devices: 11.6 us -> none  [on_device(): lax.all_to_all(buffer.reshape(devices, capacity, 256), ('lon', 'lat'), sp...]
    unnamed x27 -> x25, local copies, waits for them, and re-layouts: 2.72 us -> 1.16 us
    pallas_call x1, Pallas kernels: 17.7 us -> 19.3 us  [scatter(): pl.pallas_call(scatter_kernel, in_specs=[vm, vm], out_specs=vm, out_shape...]
  transfers between devices with their start and end apart: 1 -> 0, of which waited for: 1 -> 0; matrix products, arithmetic and copies ran while one was open for 2% -> 0% of each run, Pallas kernels for 0% -> 0%
where the time goes in v4:
time: 132 us; the launch traced here: 131 us
  Pallas kernels  124 us (94%)
  local copies, waits for them, and re-layouts  4.09 us (3%)
  other arithmetic  1.67 us (1%)
    pallas_call x1, Pallas kernels, block(): pl.pallas_call(block_kernel, in_specs=[pl.BlockSpec(memory_space=pl.ANY)]...  65 us
    pallas_call x1, Pallas kernels, ship(): pl.pallas_call(ship_kernel, in_specs=[sm, vm, vm, vm, vm], out_specs=vm,...  40.1 us
    pallas_call x1, Pallas kernels, scatter(): pl.pallas_call(scatter_kernel, in_specs=[vm, vm], out_specs=vm, out_shape...  19.3 us
    slice x1, local copies, waits for them, and re-layouts, block(): return out[:, :72]  2.73 us

profile of v4, /device:TPU:1, one launch (start us, length us, event | category | flops | bytes accessed | tf_op | source)
XLA Modules:
  0.0 131.2 jit_solution(6086451498057544580)
XLA Ops:
  0.0 0.0 copy-start.9
  0.0 0.0 copy-start.4
  0.0 0.0 copy-start.6
  0.0 0.0 copy-start.5
  0.0 0.0 copy-start
  0.8 1.1 copy.15
  2.0 0.0 slice-start
  2.0 0.2 copy.17.wqkv_ref
  2.1 1.3 %broadcast_multiply_fusion = f32[6,144,144]{2,1,0:T(8,128)S(1)} fusion(f32[6,144,144]{2,1,0:T(8,128)} %param.22), kind=kLoop, calls=%fused_computation.1 | loop fusion | flops 124416 | bytes 995328 | tf_op jit(solution)/shard_map/mul | solution.py:40
  3.5 0.0 copy-done.4
  3.5 0.0 copy-done.6
  3.5 0.0 copy-done.5
  3.5 0.0 copy-done
  3.5 0.0 slice-start.1
  3.5 40.1 %shard_map.136.recv_ref = bf16[128,56,128]{2,1,0:T(8,128)(2,1)S(1)} custom-call(s32[1]{0:T(128)S(6)} %copy.18.cnt_ref, s32[1,2048]{1,0:T(1,128)S(1)} %bitcast.19, s32[1,2048]{1,0:T(1,128)S(1)} %bitcast.20, bf16[2048,256]{1,0:T(8,128)(2,1)S(1)} %copy-done, bf16[192,256]{1,0:T(8,128)(2,1)S(1)} %bitcast.18), custom_call_target="tpu_custom_call" | custom-call | tf_op jit(solution)/shard_map/pallas_call | solution.py:188
  43.6 0.0 copy-done.9
  43.6 0.3 bitcast_add_fusion.bias_ref
  44.0 0.0 slice-done
  44.0 0.0 slice-done.1
  44.0 0.0 copy-start.1
  44.0 0.0 copy-start.2
  44.0 0.0 copy-start.3
  44.0 0.0 copy-start.7
  44.0 0.0 copy-start.8
  44.1 19.3 %shard_map.137 = bf16[10368,192]{1,0:T(8,128)(2,1)S(1)} custom-call(bf16[128,56,128]{2,1,0:T(8,128)(2,1)S(1)} %shard_map.136.recv_ref, bf16[10368,192]{1,0:T(8,128)(2,1)S(1)} %bitcast.16), custom_call_target="tpu_custom_call" | custom-call | tf_op jit(solution)/shard_map/pallas_call | solution.py:272
  63.3 0.0 copy-done.1
  63.3 0.0 copy-done.2
  63.4 0.0 copy-done.3
  63.4 0.0 copy-done.7
  63.4 0.0 copy-done.8
  63.4 65.0 %shard_map.138 = bf16[6,75,24,192]{3,2,1,0:T(8,128)(2,1)S(1)} custom-call(bf16[6,72,24,192]{3,2,1,0:T(8,128)(2,1)S(1)} %bitcast.13, f32[4,864,144]{2,1,0:T(8,128)S(1)} %bitcast_add_fusion.bias_ref, f32[1,192]{1,0:T(1,128)S(1)} %bitcast.21, bf16[192,768]{1,0:T(8,128)(2,1)S(1)} %copy.17.wqkv_ref, bf16[192,192]{1,0:T(8,128)(2,1)S(1)} %copy-done.3, ...), custom_call_target="tpu_custom_call" | custom-call | tf_op jit(solution)/shard_map/pallas_call | solution.py:507
  128.4 2.7 %slice.3 = bf16[6,72,24,192]{3,2,1,0:T(8,128)(2,1)} slice(bf16[6,75,24,192]{3,2,1,0:T(8,128)(2,1)S(1)} %shard_map.138), slice={[0:6], [0:72], [0:24], [0:192]} | slice | bytes 7962624 | tf_op jit(solution)/shard_map/slice | solution.py:530
  (2 shorter events, 0.1 us)
Async XLA Ops:
  0.0 43.6 %copy-start.9 = (f32[4,144,144]{2,1,0:T(8,128)S(1)}, f32[4,144,144]{2,1,0:T(8,128)}, u32[]{:S(2)}) copy-start(f32[4,144,144]{2,1,0:T(8,128)} %constant.7.clone) | copy-start | bytes 995332
  0.0 3.5 %copy-start.4 = (bf16[256,192]{0,1:T(8,128)(2,1)S(1)}, bf16[256,192]{0,1:T(8,128)(2,1)}, u32[]{:S(2)}) copy-start(bf16[256,192]{0,1:T(8,128)(2,1)} %param.19) | copy-start | bytes 294916
  0.0 3.5 %copy-start.6 = (s32[2048]{0:T(1024)S(1)}, s32[2048]{0:T(1024)}, u32[]{:S(2)}) copy-start(s32[2048]{0:T(1024)} %param.17) | copy-start | bytes 24580
  0.0 3.5 %copy-start.5 = (s32[2048]{0:T(1024)S(1)}, s32[2048]{0:T(1024)}, u32[]{:S(2)}) copy-start(s32[2048]{0:T(1024)} %param.16) | copy-start | bytes 24580
  0.0 3.5 %copy-start = (bf16[2048,256]{1,0:T(8,128)(2,1)S(1)}, bf16[2048,256]{1,0:T(8,128)(2,1)}, u32[]{:S(2)}) copy-start(bf16[2048,256]{1,0:T(8,128)(2,1)} %val_ref.1) | copy-start | bytes 3145732
  2.0 42.0 %slice-start = ((s8[5308416]{0:T(1024)(128)(4,1)}), s8[1114112]{0:T(1024)(128)(4,1)S(1)}, s32[]{:S(2)}) async-start(s8[5308416]{0:T(1024)(128)(4,1)} %bitcast.14), calls=%async_computation | async-start | bytes 2228224
  3.5 40.5 %slice-start.1 = ((s8[5308416]{0:T(1024)(128)(4,1)}), s8[4194304]{0:T(1024)(128)(4,1)S(1)}, s32[]{:S(2)}) async-start(s8[5308416]{0:T(1024)(128)(4,1)} %bitcast.14), calls=%async_computation.1 | async-start | bytes 8388608
  44.0 19.3 %copy-start.1 = (bf16[192,768]{1,0:T(8,128)(2,1)S(1)}, bf16[192,768]{1,0:T(8,128)(2,1)}, u32[]{:S(2)}) copy-start(bf16[192,768]{1,0:T(8,128)(2,1)} %wup_ref.1) | copy-start | bytes 884740
  44.0 19.3 %copy-start.2 = (bf16[768,192]{0,1:T(8,128)(2,1)S(1)}, bf16[768,192]{0,1:T(8,128)(2,1)}, u32[]{:S(2)}) copy-start(bf16[768,192]{0,1:T(8,128)(2,1)} %param.26) | copy-start | bytes 884740
  44.0 19.3 %copy-start.3 = (bf16[192,192]{1,0:T(8,128)(2,1)S(1)}, bf16[192,192]{1,0:T(8,128)(2,1)}, u32[]{:S(2)}) copy-start(bf16[192,192]{1,0:T(8,128)(2,1)} %wp_ref.1) | copy-start | bytes 221188
  44.0 19.3 %copy-start.7 = (f32[192]{0:T(256)S(1)}, f32[192]{0:T(256)}, u32[]{:S(2)}) copy-start(f32[192]{0:T(256)} %param.20) | copy-start | bytes 2308
  44.0 19.3 %copy-start.8 = (f32[192]{0:T(256)S(1)}, f32[192]{0:T(256)}, u32[]{:S(2)}) copy-start(f32[192]{0:T(256)} %param.24) | copy-start | bytes 2308

commit v5 on v4

--- a/solution.py
+++ b/solution.py
@@ -36,15 +36,28 @@
 GROUPS=((0,4,0),(4,2,128))
 MESH=pl.DeviceIdType.MESH
 
-def prep_bias(position_bias):
-    b=position_bias*np.float32(LOG2E)
-    lvl=np.arange(WIN)//72; row=np.arange(WIN)//12%6
-    outs=[]
-    for le in range(2):
-        for ve in range(2):
-            g=2*le*(row>=3)+ve*lvl
-            outs.append((g[:,None]!=g[None,:]).astype(np.float32)*np.float32(-1e30))
-    return (b[None]+jnp.asarray(np.stack(outs))[:,None]).reshape(4,HEADS*WIN,WIN)
+def mask_rows(axis):
+    at = lax.broadcasted_iota(jnp.int32, (WIN, WIN), axis)
+    upper = at >= 72
+    return upper, ((at >= 36) & (at < 72)) | (at >= 108)
+
+
+def fill_bias(raw_ref, bias_ref):
+    level_q, lat_q = mask_rows(0)
+    level_k, lat_k = mask_rows(1)
+    zero = jnp.zeros((WIN, WIN), F32)
+    level_cut = jnp.where(level_q != level_k, -1e30, zero)
+    lat_cut = jnp.where(lat_q != lat_k, -1e30, zero)
+    both_cut = jnp.where((level_q != level_k) | (lat_q != lat_k), -1e30, zero)
+
+    def head(h, _):
+        rows = pl.ds(pl.multiple_of(h * WIN, WIN), WIN)
+        b = raw_ref[rows, :] * np.float32(LOG2E)
+        for v, cut in enumerate((zero, level_cut, lat_cut, both_cut)):
+            bias_ref[v, rows, :] = b + cut
+        return 0
+
+    lax.fori_loop(0, HEADS, head, 0)
 
 
 CAP = 32
@@ -212,7 +225,7 @@
     sel = jnp.where(lane == 2 * group, 128.0, jnp.where(lane == 2 * group + 1, 1.0, 0.0)).astype(BF)
     for b in range(8):
         marks = recv_ref[16 * b : 16 * b + 16, 48:56, :].astype(F32).reshape(128, 128).astype(BF)
-        ids_v[:, 128 * b : 128 * b + 128] = (dot_nt(sel, marks) + 0.5).astype(jnp.int32)
+        ids_v[:, 128 * b : 128 * b + 128] = 2 * (dot_nt(sel, marks) + 0.5).astype(jnp.int32)
     cp = pltpu.make_async_copy(ids_v, ids_s, sem)
     cp.start()
 
@@ -240,13 +253,17 @@
     half = DEV // len(accs)
 
     def body(d, _):
-        for j in range(CAP):
+        for j in range(0, CAP, 2):
             for a, acc in enumerate(accs):
                 src = d + a * half
-                c = ids_s[j // 8, src * 8 + j % 8]
-                acc[pl.ds(2 * c, 2), :] = (
-                    acc[pl.ds(2 * c, 2), :] + rows[pl.ds(2 * (src * CAP + j), 2), :]
-                )
+                first = ids_s[j // 8, src * 8 + j % 8]
+                second = ids_s[(j + 1) // 8, src * 8 + (j + 1) % 8]
+                row = 2 * (src * CAP + j)
+                old = acc[pl.ds(second, 2), :]
+                new = acc[pl.ds(first, 2), :] + rows[pl.ds(row, 2), :]
+                old = jnp.where(first == second, new, old)
+                acc[pl.ds(first, 2), :] = new
+                acc[pl.ds(second, 2), :] = old + rows[pl.ds(row + 2, 2), :]
         return 0
 
     lax.fori_loop(0, half, body, 0)
@@ -287,15 +304,15 @@
     return out.reshape(tokens.shape)
 
 
-def attend(xs, qkv_ref, s_ref, p_ref, ctx_ref, bias_ref, variants, g1_ref, wqkv_ref, wp_ref, g2_ref, wup_ref, wdnt_ref):
+def attend(xs, qkv_ref, s_ref, p_ref, ctx_ref, bias_ref, variants, g1_ref, wqkv_ref, wk_ref, wp_ref, g2_ref, wup_ref, wdnt_ref):
     zero = jnp.zeros((), BF)
     count = len(variants)
     n1 = norm(xs[...], g1_ref[...])
     qkv_ref[:, 0:256] = (
         dot(n1, wqkv_ref[:, 0:256]) * np.float32(LOG2E / math.sqrt(HD))
     ).astype(BF)
-    qkv_ref[:, 256:512] = dot(n1, wqkv_ref[:, 256:512]).astype(BF)
-    qkv_ref[:, 512:768] = dot(n1, wqkv_ref[:, 512:768]).astype(BF)
+    qkv_ref[:, 256:512] = dot(n1, wk_ref[...]).astype(BF)
+    qkv_ref[:, 512:704] = dot(n1, wqkv_ref[:, 384:576]).astype(BF)
 
     def scores(w):
         sl = slice(w * WIN, (w + 1) * WIN)
@@ -341,9 +358,9 @@
 
 
 def block_kernel(
-    x_hbm, bias_ref, g1_ref, wqkv_ref, wp_ref, g2_ref, wup_ref, wdnt_ref, o_ref,
-    xe, from_right, from_left, to_right, to_left, back_left, back_right, back_lat, back_diag,
-    xs, qkv_ref, s_ref, p_ref, ctx_ref, send_sem, recv_sem, local_sem,
+    x_ref, raw_ref, g1_ref, wqkv_ref, wp_ref, g2_ref, wup_ref, wdnt_ref, o_ref,
+    near, from_right, from_left, to_right, to_left, back_left, back_right, back_lat, back_diag,
+    xs, qkv_ref, s_ref, p_ref, ctx_ref, bias_ref, wk_ref, send_sem, recv_sem,
 ):
     lon = lax.axis_index("lon")
     lat = lax.axis_index("lat")
@@ -354,19 +371,13 @@
     north = lax.rem(lat + 1, n_lat)
     south = lax.rem(lat + n_lat - 1, n_lat)
 
-    locals_ = [
-        pltpu.make_async_copy(
-            x_hbm.at[:, r0:r1], xe.at[:, r0:r1], local_sem.at[n]
-        )
-        for n, (r0, r1) in enumerate(((0, 39), (39, 72)))
-    ]
-    for copy in locals_:
-        copy.start()
-
     barrier = pltpu.get_barrier_semaphore()
     partners = ((east, lat), (west, lat), (lon, north), (lon, south), (east, south), (west, north))
     for partner in partners:
         pl.semaphore_signal(barrier, inc=1, device_id=partner, device_id_type=MESH)
+    fill_bias(raw_ref, bias_ref)
+    wk_ref[...] = pltpu.roll(wqkv_ref[:, 128:384].astype(F32), 192, 1).astype(BF)
+    qkv_ref[:, 704:768] = jnp.zeros((6 * WIN, 64), BF)
     pl.semaphore_wait(barrier, len(partners))
 
     def remote(n, src, dst, target):
@@ -376,10 +387,10 @@
         )
 
     halo = [
-        remote(0, x_hbm.at[:, 3:39, 0:8], from_right, (west, lat)),
-        remote(1, x_hbm.at[:, 39:72, 16:24], from_left.at[:, 0:33], (east, lat)),
-        remote(2, x_hbm.at[:, 0:3], xe.at[:, 72:75], (lon, south)),
-        remote(3, x_hbm.at[:, 0:3, 16:24], from_left.at[:, 33:36], (east, south)),
+        remote(0, x_ref.at[:, 3:39, 0:8], from_right, (west, lat)),
+        remote(1, x_ref.at[:, 39:72, 16:24], from_left.at[:, 0:33], (east, lat)),
+        remote(2, x_ref.at[:, 0:3], near, (lon, south)),
+        remote(3, x_ref.at[:, 0:3, 16:24], from_left.at[:, 33:36], (east, south)),
     ]
     home_east = [
         remote(4 + j, to_right.at[:, 12 * j : 12 * j + 12], back_left.at[:, 12 * j : 12 * j + 12], (east, lat))
@@ -393,7 +404,6 @@
     home_lat = remote(11, o_ref.at[:, 72:75], back_lat, (lon, north))
     for copy in halo:
         copy.start()
-    locals_[0].wait()
 
     def step(s, _):
         phase = s // 3
@@ -407,55 +417,73 @@
 
         @pl.when(s == 6)
         def _():
-            locals_[1].wait()
             for copy in halo[1:]:
                 copy.wait_recv()
 
-        def places():
+        def places(last=None):
             for w in range(6):
                 for i in range(2):
                     for r in range(6):
+                        if last is not None and last != (w % 2 == 1 and r >= 3):
+                            continue
                         level = (w // 2 * 2 + 1 + i) % 6
-                        yield level, 3 + 6 * (2 * j + w % 2) + r, w * WIN + (i * 6 + r) * 12
-
-        @pl.when(inner)
-        def _():
-            for level, row, at in places():
-                xs[at : at + 12, :] = xe[level, row].astype(F32)[6:18]
+                        row = 3 + 6 * (2 * j + w % 2) + r
+                        yield level, row, w * WIN + (i * 6 + r) * 12, r - 3
+
+        def load_inner(level, row, at, source):
+            xs[at : at + 12, :] = source[level, row].astype(F32)[6:18]
+
+        def load_left(level, row, at, source):
+            xs[at + 6 : at + 12, :] = source[level, row, 0:8].astype(F32)[0:6]
+
+        for wanted, load in ((inner, load_inner), (phase == 2, load_left)):
+            @pl.when(wanted)
+            def _(load=load):
+                for level, row, at, _ in places(False):
+                    load(level, row, at, x_ref)
+
+            @pl.when(wanted & (j < 5))
+            def _(load=load):
+                for level, row, at, _ in places(True):
+                    load(level, row, at, x_ref)
+
+            @pl.when(wanted & (j == 5))
+            def _(load=load):
+                for level, _, at, extra in places(True):
+                    load(level, extra, at, near)
 
         @pl.when(phase == 1)
         def _():
-            for level, row, at in places():
-                xs[at : at + 6, :] = xe[level, row, 16:24].astype(F32)[2:8]
+            for level, row, at, _ in places():
+                xs[at : at + 6, :] = x_ref[level, row, 16:24].astype(F32)[2:8]
                 xs[at + 6 : at + 12, :] = from_right[level, row - 3].astype(F32)[0:6]
 
         @pl.when(phase == 2)
         def _():
-            for level, row, at in places():
+            for level, row, at, _ in places():
                 xs[at : at + 6, :] = from_left[level, row - 39].astype(F32)[2:8]
-                xs[at + 6 : at + 12, :] = xe[level, row, 0:8].astype(F32)[0:6]
 
         lat_edge = ((j == 5) & (lat == n_lat - 1)).astype(jnp.int32)
         variants = [w // 4 + (2 * lat_edge if w % 2 else 0) for w in range(6)]
         attend(
             xs, qkv_ref, s_ref, p_ref, ctx_ref, bias_ref, variants,
-            g1_ref, wqkv_ref, wp_ref, g2_ref, wup_ref, wdnt_ref,
+            g1_ref, wqkv_ref, wk_ref, wp_ref, g2_ref, wup_ref, wdnt_ref,
         )
 
         @pl.when(inner)
         def _():
-            for level, row, at in places():
+            for level, row, at, _ in places():
                 o_ref[level, row, 6:18, :] = xs[at : at + 12, :].astype(BF)
 
         @pl.when(phase == 1)
         def _():
-            for level, row, at in places():
+            for level, row, at, _ in places():
                 o_ref[level, row, 18:24, :] = xs[at : at + 6, :].astype(BF)
                 to_right[level, row - 3, 0:6, :] = xs[at + 6 : at + 12, :].astype(BF)
 
         @pl.when(phase == 2)
         def _():
-            for level, row, at in places():
+            for level, row, at, _ in places():
                 to_left[level, row - 39, 2:8, :] = xs[at : at + 6, :].astype(BF)
                 o_ref[level, row, 0:6, :] = xs[at + 6 : at + 12, :].astype(BF)
 
@@ -500,17 +528,15 @@
 
 
 def block(stream, position_bias, g1, wqkv, wp, g2, wup, wdn):
-    bias = prep_bias(position_bias)
-    wq = jnp.pad(wqkv.reshape(D, 3, D), ((0, 0), (0, 0), (0, 64))).reshape(D, 768)
     vm = pl.BlockSpec(memory_space=pltpu.VMEM)
     slab = pltpu.VMEM((6, 36, 8, D), BF)
     out = pl.pallas_call(
         block_kernel,
-        in_specs=[pl.BlockSpec(memory_space=pl.ANY)] + [vm] * 7,
+        in_specs=[vm] * 8,
         out_specs=vm,
         out_shape=jax.ShapeDtypeStruct((6, 75, 24, D), BF),
         scratch_shapes=[
-            pltpu.VMEM((6, 75, 24, D), BF),
+            pltpu.VMEM((6, 3, 24, D), BF),
             slab, slab, slab, slab,
             slab, pltpu.VMEM((6, 33, 8, D), BF),
             pltpu.VMEM((6, 3, 24, D), BF), pltpu.VMEM((6, 3, 8, D), BF),
@@ -519,14 +545,15 @@
             pltpu.VMEM((2, HEADS * WIN, WIN), F32),
             pltpu.VMEM((2, HEADS * WIN, WIN), BF),
             pltpu.VMEM((6 * WIN, 256), BF),
+            pltpu.VMEM((4, HEADS * WIN, WIN), F32),
+            pltpu.VMEM((D, 256), BF),
             pltpu.SemaphoreType.DMA((12,)),
             pltpu.SemaphoreType.DMA((12,)),
-            pltpu.SemaphoreType.DMA((2,)),
         ],
         compiler_params=pltpu.CompilerParams(
-            collective_id=0, has_side_effects=True, vmem_limit_bytes=34 << 20
+            collective_id=0, has_side_effects=True, vmem_limit_bytes=32 << 20
         ),
-    )(stream, bias, g1.reshape(1, D), wq, wp, g2.reshape(1, D), wup, wdn.T)
+    )(stream, position_bias.reshape(HEADS * WIN, WIN), g1.reshape(1, D), wqkv, wp, g2.reshape(1, D), wup, wdn.T)
     return out[:, :72]
 
 

time: 132 us -> 132 us (level)
  local copies, waits for them, and re-layouts: 4.09 us -> 8.76 us
  Pallas kernels: 124 us -> 121 us
  other arithmetic: 1.67 us -> 0 us
    unnamed x25 -> x24, local copies, waits for them, and re-layouts: 1.16 us -> 6.04 us
    pallas_call x1, Pallas kernels: 19.3 us -> 16.3 us  [scatter(): pl.pallas_call(scatter_kernel, in_specs=[vm, vm], out_specs=vm, out_shape...]
    mul x1 -> x0, other arithmetic: 1.34 us -> none  [prep_bias(): b = position_bias * np.float32(LOG2E)]
where the time goes in v5:
time: 132 us; the launch traced here: 131 us
  Pallas kernels  121 us (92%)
  local copies, waits for them, and re-layouts  8.76 us (7%)
    pallas_call x1, Pallas kernels, block(): pl.pallas_call(block_kernel, in_specs=[vm] * 8, out_specs=vm, out_shape=j...  65 us
    pallas_call x1, Pallas kernels, ship(): pl.pallas_call(ship_kernel, in_specs=[sm, vm, vm, vm, vm], out_specs=vm,...  39.7 us
    pallas_call x1, Pallas kernels, scatter(): pl.pallas_call(scatter_kernel, in_specs=[vm, vm], out_specs=vm, out_shape...  16.3 us
    unnamed x24, local copies, waits for them, and re-layouts  6.04 us
    slice x1, local copies, waits for them, and re-layouts, block(): return out[:, :72]  2.72 us

profile of v5, /device:TPU:1, one launch (start us, length us, event | category | flops | bytes accessed | tf_op | source)
XLA Modules:
  0.0 130.5 jit_solution(5570816371100309737)
XLA Ops:
  0.7 0.0 copy-start.1
  0.7 1.2 copy-done.1
  1.9 0.0 copy-start.7
  1.9 0.9 copy-done.7
  2.8 0.0 copy-start.8
  2.8 0.7 copy-done.8
  3.5 0.0 copy-start.9
  3.5 0.7 copy-done.9
  4.2 39.7 %shard_map.127.recv_ref = bf16[128,56,128]{2,1,0:T(8,128)(2,1)S(1)} custom-call(s32[1]{0:T(128)S(6)} %copy.14.cnt_ref, s32[1,2048]{1,0:T(1,128)S(1)} %bitcast.14, s32[1,2048]{1,0:T(1,128)S(1)} %bitcast.15, bf16[2048,256]{1,0:T(8,128)(2,1)S(1)} %copy-done.1, bf16[192,256]{1,0:T(8,128)(2,1)S(1)} %bitcast.13), custom_call_target="tpu_custom_call" | custom-call | tf_op jit(solution)/shard_map/pallas_call | solution.py:201
  43.9 0.0 copy-start
  43.9 2.5 %copy-done = bf16[6,72,24,192]{3,2,1,0:T(8,128)(2,1)S(1)} copy-done((bf16[6,72,24,192]{3,2,1,0:T(8,128)(2,1)S(1)}, bf16[6,72,24,192]{3,2,1,0:T(8,128)(2,1)}, u32[]{:S(2)}) %copy-start) | copy-done | bytes 3981336
  46.4 0.0 copy-start.2
  46.4 0.0 copy-start.3
  46.4 0.0 copy-start.4
  46.4 0.0 copy-start.5
  46.4 0.0 copy-start.6
  46.4 0.0 copy-start.10
  46.4 0.0 copy-start.11
  46.4 16.3 %shard_map.128 = bf16[10368,192]{1,0:T(8,128)(2,1)S(1)} custom-call(bf16[128,56,128]{2,1,0:T(8,128)(2,1)S(1)} %shard_map.127.recv_ref, bf16[10368,192]{1,0:T(8,128)(2,1)S(1)} %bitcast.10), custom_call_target="tpu_custom_call" | custom-call | tf_op jit(solution)/shard_map/pallas_call | solution.py:289
  62.8 0.0 copy-done.2
  62.8 0.0 copy-done.3
  62.8 0.0 copy-done.4
  62.8 0.0 copy-done.5
  62.8 0.0 copy-done.6
  62.8 0.0 copy-done.10
  62.8 0.0 copy-done.11
  62.8 65.0 %shard_map.129 = bf16[6,75,24,192]{3,2,1,0:T(8,128)(2,1)S(1)} custom-call(bf16[6,72,24,192]{3,2,1,0:T(8,128)(2,1)S(1)} %bitcast.9, f32[864,144]{1,0:T(8,128)S(1)} %bitcast.11, f32[1,192]{1,0:T(1,128)S(1)} %bitcast.16, bf16[192,576]{1,0:T(8,128)(2,1)S(1)} %copy-done.5, bf16[192,192]{1,0:T(8,128)(2,1)S(1)} %copy-done.6, f32[1,192]{1,0:T(1,128)S(1)} %bitcast.17, ...), custom_call_target="tpu_custom_call" | custom-call | tf_op jit(solution)/shard_map/pallas_call | solution.py:533
  127.8 2.7 %slice.3 = bf16[6,72,24,192]{3,2,1,0:T(8,128)(2,1)} slice(bf16[6,75,24,192]{3,2,1,0:T(8,128)(2,1)S(1)} %shard_map.129), slice={[0:6], [0:72], [0:24], [0:192]} | slice | bytes 7962624 | tf_op jit(solution)/shard_map/slice | solution.py:557
Async XLA Ops:
  0.7 1.2 copy-start.1
  1.9 0.9 copy-start.7
  2.8 0.7 copy-start.8
  3.5 0.7 copy-start.9
  43.9 2.5 %copy-start = (bf16[6,72,24,192]{3,2,1,0:T(8,128)(2,1)S(1)}, bf16[6,72,24,192]{3,2,1,0:T(8,128)(2,1)}, u32[]{:S(2)}) copy-start(bf16[6,72,24,192]{3,2,1,0:T(8,128)(2,1)} %param.13) | copy-start | bytes 11943940
  46.4 16.4 %copy-start.2 = (f32[6,144,144]{2,1,0:T(8,128)S(1)}, f32[6,144,144]{2,1,0:T(8,128)}, u32[]{:S(2)}) copy-start(f32[6,144,144]{2,1,0:T(8,128)} %param.21) | copy-start | bytes 1492996
  46.4 16.4 %copy-start.3 = (bf16[192,768]{1,0:T(8,128)(2,1)S(1)}, bf16[192,768]{1,0:T(8,128)(2,1)}, u32[]{:S(2)}) copy-start(bf16[192,768]{1,0:T(8,128)(2,1)} %wup_ref.1) | copy-start | bytes 884740
  46.4 16.4 %copy-start.4 = (bf16[768,192]{0,1:T(8,128)(2,1)S(1)}, bf16[768,192]{0,1:T(8,128)(2,1)}, u32[]{:S(2)}) copy-start(bf16[768,192]{0,1:T(8,128)(2,1)} %param.25) | copy-start | bytes 884740
  46.4 16.4 %copy-start.5 = (bf16[192,576]{1,0:T(8,128)(2,1)S(1)}, bf16[192,576]{1,0:T(8,128)(2,1)}, u32[]{:S(2)}) copy-start(bf16[192,576]{1,0:T(8,128)(2,1)} %wqkv_ref.1) | copy-start | bytes 663556
  46.4 16.4 %copy-start.6 = (bf16[192,192]{1,0:T(8,128)(2,1)S(1)}, bf16[192,192]{1,0:T(8,128)(2,1)}, u32[]{:S(2)}) copy-start(bf16[192,192]{1,0:T(8,128)(2,1)} %wp_ref.1) | copy-start | bytes 221188
  46.4 16.4 %copy-start.10 = (f32[192]{0:T(256)S(1)}, f32[192]{0:T(256)}, u32[]{:S(2)}) copy-start(f32[192]{0:T(256)} %param.19) | copy-start | bytes 2308
  46.4 16.4 %copy-start.11 = (f32[192]{0:T(256)S(1)}, f32[192]{0:T(256)}, u32[]{:S(2)}) copy-start(f32[192]{0:T(256)} %param.23) | copy-start | bytes 2308

commit v6 on v5

--- a/solution.py
+++ b/solution.py
@@ -68,8 +68,8 @@
 
 
 def ship_kernel(
-    cnt_ref, dest_ref, cell_ref, val_ref, wt_ref, o_ref, y_ref, slot_ref, acc_ref, buf_ref,
-    send_sem, recv_sem, local_sem,
+    cnt_ref, dest_hbm, cell_hbm, val_hbm, wt_hbm, o_ref, y_ref, slot_ref, acc_ref, buf_ref,
+    dest_ref, cell_ref, val_ref, wt_ref, send_sem, recv_sem, local_sem, load_sem,
 ):
     n_lat = lax.axis_size("lat")
     n = lax.axis_size("lon") * n_lat
@@ -79,6 +79,14 @@
     def at(device):
         return (device // n_lat, lax.rem(device, n_lat))
 
+    loads = [
+        pltpu.make_async_copy(src, dst, load_sem.at[i])
+        for i, (src, dst) in enumerate(
+            ((val_hbm, val_ref), (wt_hbm, wt_ref), (cell_hbm, cell_ref), (dest_hbm, dest_ref))
+        )
+    ]
+    for load in loads:
+        load.start()
     barrier = pltpu.get_barrier_semaphore()
 
     def greet(i, _):
@@ -88,6 +96,8 @@
         return 0
 
     lax.fori_loop(1, n, greet, 0)
+    for load in loads:
+        load.wait()
 
     eye = (
         lax.broadcasted_iota(jnp.int32, (8, 64), 0) == lax.broadcasted_iota(jnp.int32, (8, 64), 1)
@@ -198,9 +208,10 @@
     rows = values.shape[0]
     sm = pl.BlockSpec(memory_space=pltpu.SMEM)
     vm = pl.BlockSpec(memory_space=pltpu.VMEM)
+    hbm = pl.BlockSpec(memory_space=pltpu.HBM)
     return pl.pallas_call(
         ship_kernel,
-        in_specs=[sm, vm, vm, vm, vm],
+        in_specs=[sm, hbm, hbm, hbm, hbm],
         out_specs=vm,
         out_shape=jax.ShapeDtypeStruct((DEV, BLK, 128), BF),
         scratch_shapes=[
@@ -208,9 +219,14 @@
             pltpu.VMEM((1, rows), jnp.int32),
             pltpu.VMEM((CHUNK * CAP, 256), F32),
             pltpu.VMEM((DEV, BLK, 128), BF),
+            pltpu.VMEM((1, rows), jnp.int32),
+            pltpu.VMEM((1, rows), jnp.int32),
+            pltpu.VMEM(values.shape, BF),
+            pltpu.VMEM((D, values.shape[1]), BF),
             pltpu.SemaphoreType.DMA((DEV,)),
             pltpu.SemaphoreType.DMA((DEV,)),
             pltpu.SemaphoreType.DMA,
+            pltpu.SemaphoreType.DMA((4,)),
         ],
         compiler_params=pltpu.CompilerParams(
             collective_id=1, has_side_effects=True, vmem_limit_bytes=20 << 20
@@ -218,7 +234,9 @@
     )(obs_count, obs_dest.reshape(1, rows), obs_cell.reshape(1, rows), values, w_obs.T)
 
 
-def scatter_kernel(recv_ref, tok_ref, out_ref, rows, ids_v, ids_s, sem, *accs):
+def scatter_kernel(recv_ref, tok_hbm, out_ref, tok_ref, tok_sem, rows, ids_v, ids_s, sem, *accs):
+    fetch = pltpu.make_async_copy(tok_hbm, tok_ref, tok_sem)
+    fetch.start()
     cells = tok_ref.shape[0]
     group = lax.broadcasted_iota(jnp.int32, (8, 128), 0)
     lane = lax.broadcasted_iota(jnp.int32, (8, 128), 1)
@@ -238,14 +256,20 @@
         return 0
 
     lax.fori_loop(0, DEV, prep, 0, unroll=4)
+    for acc in accs[1:]:
+
+        def clear(g, _, acc=acc):
+            acc[pl.ds(pl.multiple_of(g * 288, 288), 288), :] = jnp.zeros((288, 128), F32)
+            return 0
+
+        lax.fori_loop(0, cells // 144, clear, 0)
+    fetch.wait()
 
     def init(g, _):
         r = pl.multiple_of(g * 144, 144)
         t = tok_ref[pl.ds(r, 144), :].astype(F32)
         accs[0][pl.ds(2 * r, 144, stride=2), :] = t[:, 0:128]
         accs[0][pl.ds(2 * r + 1, 144, stride=2), 0:64] = t[:, 128:192]
-        for a in accs[1:]:
-            a[pl.ds(2 * r, 288), :] = jnp.zeros((288, 128), F32)
         return 0
 
     lax.fori_loop(0, cells // 144, init, 0)
@@ -288,10 +312,12 @@
     vm = pl.BlockSpec(memory_space=pltpu.VMEM)
     out = pl.pallas_call(
         scatter_kernel,
-        in_specs=[vm, vm],
+        in_specs=[vm, pl.BlockSpec(memory_space=pltpu.HBM)],
         out_specs=vm,
         out_shape=jax.ShapeDtypeStruct((cells, D), BF),
         scratch_shapes=[
+            pltpu.VMEM((cells, D), BF),
+            pltpu.SemaphoreType.DMA,
             pltpu.VMEM((2 * DEV * CAP, 128), F32),
             pltpu.VMEM((8, 1024), jnp.int32),
             pltpu.SMEM((8, 1024), jnp.int32),
@@ -299,7 +325,7 @@
             pltpu.VMEM((2 * cells, 128), F32),
             pltpu.VMEM((2 * cells, 128), F32),
         ],
-        compiler_params=pltpu.CompilerParams(vmem_limit_bytes=30 << 20),
+        compiler_params=pltpu.CompilerParams(vmem_limit_bytes=36 << 20),
     )(recv, tokens.reshape(cells, D))
     return out.reshape(tokens.shape)
 

time: 132 us -> 133 us (level)
  no operation moved by 1% of the time
where the time goes in v6:
time: 133 us; the launch traced here: 132 us
  Pallas kernels  122 us (92%)
  local copies, waits for them, and re-layouts  8.76 us (7%)
    pallas_call x1, Pallas kernels, block(): pl.pallas_call(block_kernel, in_specs=[vm] * 8, out_specs=vm, out_shape=j...  65 us
    pallas_call x1, Pallas kernels, ship(): pl.pallas_call(ship_kernel, in_specs=[sm, hbm, hbm, hbm, hbm], out_specs=...  40.2 us
    pallas_call x1, Pallas kernels, scatter(): pl.pallas_call(scatter_kernel, in_specs=[vm, pl.BlockSpec(memory_space=pl...  17 us
    unnamed x24, local copies, waits for them, and re-layouts  6.04 us
    slice x1, local copies, waits for them, and re-layouts, block(): return out[:, :72]  2.72 us

profile of v6, /device:TPU:1, one launch (start us, length us, event | category | flops | bytes accessed | tf_op | source)
XLA Modules:
  0.0 131.7 jit_solution(8344260672260572897)
XLA Ops:
  0.7 0.0 copy-start.1
  0.7 1.2 copy-done.1
  1.9 0.0 copy-start.7
  1.9 0.9 copy-done.7
  2.8 0.0 copy-start.8
  2.8 0.7 copy-done.8
  3.5 0.0 copy-start.9
  3.5 0.7 copy-done.9
  4.2 40.2 %shard_map.127.recv_ref = bf16[128,56,128]{2,1,0:T(8,128)(2,1)S(1)} custom-call(s32[1]{0:T(128)S(6)} %copy.14.cnt_ref, s32[1,2048]{1,0:T(1,128)S(1)} %bitcast.14, s32[1,2048]{1,0:T(1,128)S(1)} %bitcast.15, bf16[2048,256]{1,0:T(8,128)(2,1)S(1)} %copy-done.1, bf16[192,256]{1,0:T(8,128)(2,1)S(1)} %bitcast.13), custom_call_target="tpu_custom_call" | custom-call | tf_op jit(solution)/shard_map/pallas_call | solution.py:212
  44.4 0.0 copy-start
  44.4 2.5 %copy-done = bf16[6,72,24,192]{3,2,1,0:T(8,128)(2,1)S(1)} copy-done((bf16[6,72,24,192]{3,2,1,0:T(8,128)(2,1)S(1)}, bf16[6,72,24,192]{3,2,1,0:T(8,128)(2,1)}, u32[]{:S(2)}) %copy-start) | copy-done | bytes 3981336
  46.9 0.0 copy-start.2
  46.9 0.0 copy-start.3
  46.9 0.0 copy-start.4
  46.9 0.0 copy-start.5
  46.9 0.0 copy-start.6
  46.9 0.0 copy-start.10
  46.9 0.0 copy-start.11
  47.0 17.0 %shard_map.128 = bf16[10368,192]{1,0:T(8,128)(2,1)S(1)} custom-call(bf16[128,56,128]{2,1,0:T(8,128)(2,1)S(1)} %shard_map.127.recv_ref, bf16[10368,192]{1,0:T(8,128)(2,1)S(1)} %bitcast.10), custom_call_target="tpu_custom_call" | custom-call | tf_op jit(solution)/shard_map/pallas_call | solution.py:313
  64.0 0.0 copy-done.2
  64.0 0.0 copy-done.3
  64.0 0.0 copy-done.4
  64.0 0.0 copy-done.5
  64.0 0.0 copy-done.6
  64.0 0.0 copy-done.10
  64.0 0.0 copy-done.11
  64.1 65.0 %shard_map.129 = bf16[6,75,24,192]{3,2,1,0:T(8,128)(2,1)S(1)} custom-call(bf16[6,72,24,192]{3,2,1,0:T(8,128)(2,1)S(1)} %bitcast.9, f32[864,144]{1,0:T(8,128)S(1)} %bitcast.11, f32[1,192]{1,0:T(1,128)S(1)} %bitcast.16, bf16[192,576]{1,0:T(8,128)(2,1)S(1)} %copy-done.5, bf16[192,192]{1,0:T(8,128)(2,1)S(1)} %copy-done.6, f32[1,192]{1,0:T(1,128)S(1)} %bitcast.17, ...), custom_call_target="tpu_custom_call" | custom-call | tf_op jit(solution)/shard_map/pallas_call | solution.py:559
  129.0 2.7 %slice.3 = bf16[6,72,24,192]{3,2,1,0:T(8,128)(2,1)} slice(bf16[6,75,24,192]{3,2,1,0:T(8,128)(2,1)S(1)} %shard_map.129), slice={[0:6], [0:72], [0:24], [0:192]} | slice | bytes 7962624 | tf_op jit(solution)/shard_map/slice | solution.py:583
Async XLA Ops:
  0.7 1.2 copy-start.1
  1.9 0.9 copy-start.7
  2.8 0.7 copy-start.8
  3.5 0.7 copy-start.9
  44.4 2.5 %copy-start = (bf16[6,72,24,192]{3,2,1,0:T(8,128)(2,1)S(1)}, bf16[6,72,24,192]{3,2,1,0:T(8,128)(2,1)}, u32[]{:S(2)}) copy-start(bf16[6,72,24,192]{3,2,1,0:T(8,128)(2,1)} %param.13) | copy-start | bytes 11943940
  46.9 17.1 %copy-start.2 = (f32[6,144,144]{2,1,0:T(8,128)S(1)}, f32[6,144,144]{2,1,0:T(8,128)}, u32[]{:S(2)}) copy-start(f32[6,144,144]{2,1,0:T(8,128)} %param.21) | copy-start | bytes 1492996
  46.9 17.1 %copy-start.3 = (bf16[192,768]{1,0:T(8,128)(2,1)S(1)}, bf16[192,768]{1,0:T(8,128)(2,1)}, u32[]{:S(2)}) copy-start(bf16[192,768]{1,0:T(8,128)(2,1)} %wup_ref.1) | copy-start | bytes 884740
  46.9 17.1 %copy-start.4 = (bf16[768,192]{0,1:T(8,128)(2,1)S(1)}, bf16[768,192]{0,1:T(8,128)(2,1)}, u32[]{:S(2)}) copy-start(bf16[768,192]{0,1:T(8,128)(2,1)} %param.25) | copy-start | bytes 884740
  46.9 17.1 %copy-start.5 = (bf16[192,576]{1,0:T(8,128)(2,1)S(1)}, bf16[192,576]{1,0:T(8,128)(2,1)}, u32[]{:S(2)}) copy-start(bf16[192,576]{1,0:T(8,128)(2,1)} %wqkv_ref.1) | copy-start | bytes 663556
  46.9 17.1 %copy-start.6 = (bf16[192,192]{1,0:T(8,128)(2,1)S(1)}, bf16[192,192]{1,0:T(8,128)(2,1)}, u32[]{:S(2)}) copy-start(bf16[192,192]{1,0:T(8,128)(2,1)} %wp_ref.1) | copy-start | bytes 221188
  46.9 17.1 %copy-start.10 = (f32[192]{0:T(256)S(1)}, f32[192]{0:T(256)}, u32[]{:S(2)}) copy-start(f32[192]{0:T(256)} %param.19) | copy-start | bytes 2308
  46.9 17.1 %copy-start.11 = (f32[192]{0:T(256)S(1)}, f32[192]{0:T(256)}, u32[]{:S(2)}) copy-start(f32[192]{0:T(256)} %param.23) | copy-start | bytes 2308

commit v7 on v6

--- a/solution.py
+++ b/solution.py
@@ -229,7 +229,7 @@
             pltpu.SemaphoreType.DMA((4,)),
         ],
         compiler_params=pltpu.CompilerParams(
-            collective_id=1, has_side_effects=True, vmem_limit_bytes=20 << 20
+            collective_id=1, has_side_effects=True, vmem_limit_bytes=62_000_000
         ),
     )(obs_count, obs_dest.reshape(1, rows), obs_cell.reshape(1, rows), values, w_obs.T)
 

time: 133 us -> 132 us (level)
  local copies, waits for them, and re-layouts: 8.76 us -> 6.76 us
    unnamed x24 -> x18, local copies, waits for them, and re-layouts: 6.04 us -> 4.03 us
where the time goes in v7:
time: 132 us; the launch traced here: 131 us
  Pallas kernels  123 us (93%)
  local copies, waits for them, and re-layouts  6.76 us (5%)
    pallas_call x1, Pallas kernels, block(): pl.pallas_call(block_kernel, in_specs=[vm] * 8, out_specs=vm, out_shape=j...  65 us
    pallas_call x1, Pallas kernels, ship(): pl.pallas_call(ship_kernel, in_specs=[sm, hbm, hbm, hbm, hbm], out_specs=...  41.3 us
    pallas_call x1, Pallas kernels, scatter(): pl.pallas_call(scatter_kernel, in_specs=[vm, pl.BlockSpec(memory_space=pl...  17 us
    unnamed x18, local copies, waits for them, and re-layouts  4.03 us
    slice x1, local copies, waits for them, and re-layouts, block(): return out[:, :72]  2.72 us

profile of v7, /device:TPU:1, one launch (start us, length us, event | category | flops | bytes accessed | tf_op | source)
XLA Modules:
  0.0 130.8 jit_solution(14385326340872508619)
XLA Ops:
  0.7 41.3 %shard_map.127.recv_ref = bf16[128,56,128]{2,1,0:T(8,128)(2,1)} custom-call(s32[1]{0:T(128)S(6)} %copy.14.cnt_ref, s32[1,2048]{1,0:T(1,128)} %bitcast.16, s32[1,2048]{1,0:T(1,128)} %bitcast.17, bf16[2048,256]{1,0:T(8,128)(2,1)} %val_hbm.1, bf16[192,256]{1,0:T(8,128)(2,1)} %bitcast.15), custom_call_target="tpu_custom_call" | custom-call | tf_op jit(solution)/shard_map/pallas_call | solution.py:212
  42.0 0.0 copy-start
  42.0 1.5 %copy-done = bf16[128,56,128]{2,1,0:T(8,128)(2,1)S(1)} copy-done((bf16[128,56,128]{2,1,0:T(8,128)(2,1)S(1)}, bf16[128,56,128]{2,1,0:T(8,128)(2,1)}, u32[]{:S(2)}) %copy-start) | copy-done | bytes 1835032
  43.5 0.0 copy-start.1
  43.5 2.5 %copy-done.1 = bf16[6,72,24,192]{3,2,1,0:T(8,128)(2,1)S(1)} copy-done((bf16[6,72,24,192]{3,2,1,0:T(8,128)(2,1)S(1)}, bf16[6,72,24,192]{3,2,1,0:T(8,128)(2,1)}, u32[]{:S(2)}) %copy-start.1) | copy-done | bytes 3981336
  46.0 0.0 copy-start.2
  46.0 0.0 copy-start.3
  46.0 0.0 copy-start.4
  46.0 0.0 copy-start.5
  46.0 0.0 copy-start.6
  46.0 0.0 copy-start.7
  46.0 0.0 copy-start.8
  46.0 17.0 %shard_map.128 = bf16[10368,192]{1,0:T(8,128)(2,1)S(1)} custom-call(bf16[128,56,128]{2,1,0:T(8,128)(2,1)S(1)} %copy-done, bf16[10368,192]{1,0:T(8,128)(2,1)S(1)} %bitcast.10), custom_call_target="tpu_custom_call" | custom-call | tf_op jit(solution)/shard_map/pallas_call | solution.py:313
  63.1 0.0 copy-done.2
  63.1 0.0 copy-done.3
  63.1 0.0 copy-done.4
  63.1 0.0 copy-done.5
  63.1 0.0 copy-done.6
  63.1 0.0 copy-done.7
  63.1 0.0 copy-done.8
  63.2 65.0 %shard_map.129 = bf16[6,75,24,192]{3,2,1,0:T(8,128)(2,1)S(1)} custom-call(bf16[6,72,24,192]{3,2,1,0:T(8,128)(2,1)S(1)} %bitcast.9, f32[864,144]{1,0:T(8,128)S(1)} %bitcast.11, f32[1,192]{1,0:T(1,128)S(1)} %bitcast.13, bf16[192,576]{1,0:T(8,128)(2,1)S(1)} %copy-done.5, bf16[192,192]{1,0:T(8,128)(2,1)S(1)} %copy-done.6, f32[1,192]{1,0:T(1,128)S(1)} %bitcast.14, ...), custom_call_target="tpu_custom_call" | custom-call | tf_op jit(solution)/shard_map/pallas_call | solution.py:559
  128.1 2.7 %slice.3 = bf16[6,72,24,192]{3,2,1,0:T(8,128)(2,1)} slice(bf16[6,75,24,192]{3,2,1,0:T(8,128)(2,1)S(1)} %shard_map.129), slice={[0:6], [0:72], [0:24], [0:192]} | slice | bytes 7962624 | tf_op jit(solution)/shard_map/slice | solution.py:583
Async XLA Ops:
  42.0 1.5 %copy-start = (bf16[128,56,128]{2,1,0:T(8,128)(2,1)S(1)}, bf16[128,56,128]{2,1,0:T(8,128)(2,1)}, u32[]{:S(2)}) copy-start(bf16[128,56,128]{2,1,0:T(8,128)(2,1)} %shard_map.127.recv_ref) | copy-start | bytes 5505028
  43.5 2.5 %copy-start.1 = (bf16[6,72,24,192]{3,2,1,0:T(8,128)(2,1)S(1)}, bf16[6,72,24,192]{3,2,1,0:T(8,128)(2,1)}, u32[]{:S(2)}) copy-start(bf16[6,72,24,192]{3,2,1,0:T(8,128)(2,1)} %param.13) | copy-start | bytes 11943940
  46.0 17.1 %copy-start.2 = (f32[6,144,144]{2,1,0:T(8,128)S(1)}, f32[6,144,144]{2,1,0:T(8,128)}, u32[]{:S(2)}) copy-start(f32[6,144,144]{2,1,0:T(8,128)} %param.21) | copy-start | bytes 1492996
  46.0 17.1 %copy-start.3 = (bf16[192,768]{1,0:T(8,128)(2,1)S(1)}, bf16[192,768]{1,0:T(8,128)(2,1)}, u32[]{:S(2)}) copy-start(bf16[192,768]{1,0:T(8,128)(2,1)} %wup_ref.1) | copy-start | bytes 884740
  46.0 17.1 %copy-start.4 = (bf16[768,192]{0,1:T(8,128)(2,1)S(1)}, bf16[768,192]{0,1:T(8,128)(2,1)}, u32[]{:S(2)}) copy-start(bf16[768,192]{0,1:T(8,128)(2,1)} %param.25) | copy-start | bytes 884740
  46.0 17.1 %copy-start.5 = (bf16[192,576]{1,0:T(8,128)(2,1)S(1)}, bf16[192,576]{1,0:T(8,128)(2,1)}, u32[]{:S(2)}) copy-start(bf16[192,576]{1,0:T(8,128)(2,1)} %wqkv_ref.1) | copy-start | bytes 663556
  46.0 17.1 %copy-start.6 = (bf16[192,192]{1,0:T(8,128)(2,1)S(1)}, bf16[192,192]{1,0:T(8,128)(2,1)}, u32[]{:S(2)}) copy-start(bf16[192,192]{1,0:T(8,128)(2,1)} %wp_ref.1) | copy-start | bytes 221188
  46.0 17.1 %copy-start.7 = (f32[192]{0:T(256)S(1)}, f32[192]{0:T(256)}, u32[]{:S(2)}) copy-start(f32[192]{0:T(256)} %param.19) | copy-start | bytes 2308
  46.0 17.1 %copy-start.8 = (f32[192]{0:T(256)S(1)}, f32[192]{0:T(256)}, u32[]{:S(2)}) copy-start(f32[192]{0:T(256)} %param.23) | copy-start | bytes 2308
